TPU v7x, 512 devices: a whole 4x8x8 slice. The times are simulated.
512 devices in a mesh: ctx: 64 (over z, x, core), head: 8 (over y).
Axes of the slice: x: 4, y: 8, z: 8, core: 2. Of those that a mesh axis runs over, the one named last changes fastest.
Arguments:
- queries: bfloat16 [24576, 64, 128], P(('ctx', 'head')), may hold values from -6 to 6
- keys: bfloat16 [24576, 64, 128], P(('ctx', 'head')), may hold values from -6 to 6
- values: bfloat16 [24576, 64, 128], P(('ctx', 'head')), may hold values from -6 to 6
- decay_log: bfloat16 [24576, 64], P(('ctx', 'head')), may hold values from -1 to 0, as said below
- out_gain: float32 [64, 128], replicated, may hold values from 0.1 to 1.9
Outputs:
- normed: bfloat16 [24576, 64, 128], P(('ctx', 'head'))
Inputs may be any that keep to these rules, and one draw needn't show every extreme that they name: `decay_log`: every entry is negative or zero.
All inputs are finite; a program needn't handle non-finite values.
Results may differ from a plain program's by a relative error of at most 0.01.
Values may be sent and summed in bfloat16 or wider, within the bound.
No kernel may reach another device: no remote copies, remote signals or barrier semaphores. Data moves between devices by JAX's collectives and lax.ppermute only.
A program may use at most 128 MiB of HBM per device.

v0:
```python
import functools

import jax
import jax.numpy as jnp
from jax import lax
from jax.experimental import pallas as pl
from jax.experimental.pallas import tpu as pltpu
from jax.sharding import Mesh
from jax.sharding import PartitionSpec as P

F32 = jnp.float32
BF16 = jnp.bfloat16
GROUP = 16
EXTRA = 8
LIMIT = 16 * 1024 * 1024
FULL = 60 * 1024 * 1024


def iota(shape, axis):
    return lax.broadcasted_iota(jnp.int32, shape, axis)


def silu(x):
    half = 0.5 * x
    return half + half * jnp.tanh(half)


def three_parts(x):
    high = x.astype(BF16)
    rest = x - high.astype(F32)
    middle = rest.astype(BF16)
    low = (rest - middle.astype(F32)).astype(BF16)
    return high, middle, low


def dot_parts(mask, parts):
    return sum(jnp.dot(mask, part, preferred_element_type=F32) for part in parts)


def cumulative(decay):
    tokens, heads = decay.shape
    tril = (iota((tokens, tokens), 0) >= iota((tokens, tokens), 1)).astype(F32).astype(BF16)
    running = jnp.dot(tril, decay, preferred_element_type=F32)
    return jnp.concatenate([running, jnp.zeros((tokens, 128 - heads), F32)], axis=1)


def group_lanes(x, head):
    return pltpu.roll(x, lax.rem(128 - head, 128), 1)


def pack_kv_kernel(
    decay_hbm, keys_hbm, values_hbm, out_hbm,
    decay, keys, values, key_rows, value_rows, to_end, totals, out, decay_sem, in_sem, out_sem,
):
    tokens, heads, _ = keys.shape
    groups = heads // GROUP

    def copies_in(g):
        columns = pl.ds(g * GROUP, GROUP)
        return [
            pltpu.make_async_copy(source.at[:, columns, :], target.at[:, columns, :], in_sem.at[i, g])
            for i, (source, target) in enumerate(((keys_hbm, keys), (values_hbm, values)))
        ]

    def copy_out(g):
        here = pl.ds(g * GROUP, GROUP)
        return pltpu.make_async_copy(out.at[here], out_hbm.at[here], out_sem.at[g])

    decay_copy = pltpu.make_async_copy(decay_hbm, decay, decay_sem)
    decay_copy.start()
    for g in range(groups):
        for copy in copies_in(g):
            copy.start()
    decay_copy.wait()
    running = cumulative(decay[...])
    to_end[...] = jnp.exp(running[tokens - 1 : tokens, :] - running)
    row = iota((EXTRA, 128), 0)
    total = jnp.broadcast_to(running[tokens - 1 : tokens, :], (EXTRA, 128))
    high, middle, low = (part.astype(F32) for part in three_parts(total))
    totals[...] = jnp.where(row == 0, high, jnp.where(row == 1, middle, jnp.where(row == 2, low, 0.0)))

    def one(g, carry):
        for copy in copies_in(g):
            copy.wait()
        columns = pl.ds(g * GROUP, GROUP)
        scales, ends = group_lanes(to_end[...], g * GROUP), group_lanes(totals[...], g * GROUP)
        key_rows[...] = keys[:, columns, :].astype(F32).reshape(tokens * GROUP, 128)
        value_rows[...] = values[:, columns, :].astype(F32).reshape(tokens * GROUP, 128)
        for j in range(GROUP):
            rows = pl.ds(j, tokens, stride=GROUP)
            head = g * GROUP + j
            scale = jnp.broadcast_to(scales[:, j : j + 1], (tokens, 128))
            out[head, 0:tokens, :] = (silu(key_rows[rows, :]) * scale).astype(BF16)
            out[head, tokens : 2 * tokens, :] = silu(value_rows[rows, :]).astype(BF16)
            end = jnp.broadcast_to(ends[:, j : j + 1], (EXTRA, 128))
            out[head, 2 * tokens : 2 * tokens + EXTRA, :] = end.astype(BF16)
        copy_out(g).start()
        return carry

    lax.fori_loop(0, groups, one, 0)
    for g in range(groups):
        copy_out(g).wait()


def pack_kv(keys, values, decay):
    tokens, heads, dim = keys.shape
    anywhere = pl.BlockSpec(memory_space=pl.ANY)
    packed = (heads, 2 * tokens + EXTRA, dim)
    return pl.pallas_call(
        pack_kv_kernel,
        in_specs=[anywhere] * 3,
        out_specs=anywhere,
        out_shape=jax.ShapeDtypeStruct(packed, BF16),
        scratch_shapes=[
            pltpu.VMEM(decay.shape, BF16),
            pltpu.VMEM(keys.shape, BF16),
            pltpu.VMEM(values.shape, BF16),
            pltpu.VMEM((tokens * GROUP, dim), F32),
            pltpu.VMEM((tokens * GROUP, dim), F32),
            pltpu.VMEM((tokens, 128), F32),
            pltpu.VMEM((EXTRA, 128), F32),
            pltpu.VMEM(packed, BF16),
            pltpu.SemaphoreType.DMA,
            pltpu.SemaphoreType.DMA((2, heads // GROUP)),
            pltpu.SemaphoreType.DMA((heads // GROUP,)),
        ],
        compiler_params=pltpu.CompilerParams(vmem_limit_bytes=FULL),
        name="pack_kv",
    )(decay, keys, values)


def pack_q_kernel(decay_ref, queries_ref, out_ref, query_rows):
    tokens = queries_ref.shape[0]
    running = group_lanes(cumulative(decay_ref[...]), 8 * pl.program_id(0))
    query_rows[...] = queries_ref[...].astype(F32).reshape(tokens * 8, 128)
    grown = jnp.exp(running)
    for j in range(8):
        scale = jnp.broadcast_to(grown[:, j : j + 1], (tokens, 128))
        rows = query_rows[pl.ds(j, tokens, stride=8), :]
        out_ref[j] = (silu(rows) * scale).astype(BF16)


def pack_q(queries, decay):
    tokens, heads, dim = queries.shape
    return pl.pallas_call(
        pack_q_kernel,
        grid=(heads // 8,),
        in_specs=[
            pl.BlockSpec((tokens, heads), lambda g: (0, 0)),
            pl.BlockSpec((tokens, 8, dim), lambda g: (0, g, 0)),
        ],
        out_specs=pl.BlockSpec((8, tokens, dim), lambda g: (g, 0, 0)),
        out_shape=jax.ShapeDtypeStruct((heads, tokens, dim), BF16),
        scratch_shapes=[pltpu.VMEM((tokens * 8, dim), F32)],
        compiler_params=pltpu.CompilerParams(vmem_limit_bytes=LIMIT),
        name="pack_q",
    )(decay, queries)


def states_kernel(per_block, kv_ref, prefix_ref, total_ref, decay_ref, factor_ref, enter_ref, reach_ref):
    sources, rows, dim = kv_ref.shape
    tokens = (rows - EXTRA) // 2
    blocks = sources // per_block
    length = per_block * tokens
    tail = kv_ref[:, 2 * tokens : rows, :].astype(F32)
    totals = jnp.sum(tail, axis=1)
    parts = three_parts(totals)
    at, of = iota((sources, sources), 0), iota((sources, sources), 1)
    same = at // per_block == of // per_block

    def mask(keep):
        return keep.astype(F32).astype(BF16)

    before = dot_parts(mask(same & (of < at)), parts)
    after = dot_parts(mask(same & (of > at)), parts)
    enter_ref[...] = jnp.exp(before)
    to_block_end = jnp.exp(after)
    block_at, source_of = iota((blocks, sources), 0), iota((blocks, sources), 1) // per_block
    block_total = dot_parts(mask(block_at == source_of), parts)
    block_before = dot_parts(mask(block_at > source_of), parts)
    reach_ref[...] = jnp.exp(block_before)
    in_lanes = jnp.transpose(totals)[0:blocks, :]
    picked = jnp.where(block_at == source_of, in_lanes, 0.0)
    member, position = iota((sources, length), 0), iota((sources, length), 1)
    up_to = mask(lax.rem(member, per_block) <= position // tokens)
    through = sum(jnp.dot(part, up_to, preferred_element_type=F32) for part in three_parts(picked))
    source_row = iota((per_block, length), 0)
    source_col = iota((per_block, length), 1) // tokens
    repeats = length // dim
    state = jnp.zeros((dim, dim), F32)
    for b in range(blocks):
        here = slice(b * per_block, (b + 1) * per_block)
        start = jnp.concatenate([before[here]] * repeats, axis=1)
        factor_ref[b] = jnp.where(
            source_col <= source_row, jnp.exp(start - through[b : b + 1, :]), 0.0
        )
        prefix_ref[b] = state
        keys = kv_ref[here, 0:tokens, :].astype(F32) * to_block_end[here][:, None, :]
        values = kv_ref[here, tokens : 2 * tokens, :].reshape(length, dim)
        own = lax.dot_general(
            keys.astype(BF16).reshape(length, dim), values, (((0,), (0,)), ((), ())),
            preferred_element_type=F32,
        )
        state = jnp.exp(block_total[b : b + 1, :]) * state + own
    total_ref[...] = state
    decay_ref[...] = jnp.exp(jnp.sum(block_total, axis=0, keepdims=True))


def states(kv, per_block):
    sources, rows, dim = kv.shape
    blocks, length = sources // per_block, per_block * (rows - EXTRA) // 2
    return pl.pallas_call(
        functools.partial(states_kernel, per_block),
        out_shape=(
            jax.ShapeDtypeStruct((blocks, dim, dim), F32),
            jax.ShapeDtypeStruct((dim, dim), F32),
            jax.ShapeDtypeStruct((1, dim), F32),
            jax.ShapeDtypeStruct((blocks, per_block, length), F32),
            jax.ShapeDtypeStruct((sources, dim), F32),
            jax.ShapeDtypeStruct((blocks, dim), F32),
        ),
        compiler_params=pltpu.CompilerParams(vmem_limit_bytes=LIMIT),
        name="states",
    )(kv)


def attend_kernel(query_ref, kv_ref, prefix_ref, factor_ref, enter_ref, reach_ref, incoming_ref, out_ref):
    sources, tokens, dim = query_ref.shape
    blocks = prefix_ref.shape[0]
    per_block = sources // blocks
    length = per_block * tokens
    step = 128
    causal = iota((step, step), 0) >= iota((step, step), 1)

    def spread(x):
        return jnp.concatenate(
            [jnp.broadcast_to(x[i : i + 1], (tokens, x.shape[1])) for i in range(per_block)], axis=0
        )

    def weights(b):
        here = slice(b * per_block, (b + 1) * per_block)
        query = query_ref[here].reshape(length, dim)
        key = kv_ref[here, 0:tokens, :].reshape(length, dim)
        factor = spread(factor_ref[b])
        tiles = []
        for low in range(0, length, step):
            high = low + step
            scores = lax.dot_general(
                query[low:high], key[0:high], (((1,), (1,)), ((), ())), preferred_element_type=F32
            )
            scores = scores * factor[low:high, 0:high]
            diagonal = jnp.where(causal, scores[:, low:high], 0.0)
            if low:
                diagonal = jnp.concatenate([scores[:, 0:low], diagonal], axis=1)
            tiles.append(diagonal.astype(BF16))
        return tiles

    def finish(b, tiles):
        here = slice(b * per_block, (b + 1) * per_block)
        query = query_ref[here].reshape(length, dim)
        value = kv_ref[here, tokens : 2 * tokens, :].reshape(length, dim)
        state = prefix_ref[b] + reach_ref[b : b + 1, :] * incoming_ref[...]
        inter = jnp.dot(query, state.astype(BF16), preferred_element_type=F32)
        enter = spread(enter_ref[here])
        for low in range(0, length, step):
            high = low + step
            intra = jnp.dot(tiles[low // step], value[0:high], preferred_element_type=F32)
            mixed = (intra + enter[low:high] * inter[low:high]).astype(BF16)
            for i in range(low // 16, high // 16):
                source, row = divmod(i * 16, tokens)
                piece = mixed[i * 16 - low : i * 16 - low + 16]
                out_ref[b * per_block + source, row : row + 16, :] = piece

    tiles = weights(0)
    for b in range(blocks):
        following = weights(b + 1) if b + 1 < blocks else None
        finish(b, tiles)
        tiles = following


def attend(query, kv, prefix, factor, enter, reach, incoming):
    return pl.pallas_call(
        attend_kernel,
        out_shape=jax.ShapeDtypeStruct(query.shape, BF16),
        compiler_params=pltpu.CompilerParams(vmem_limit_bytes=LIMIT),
        name="attend",
    )(query, kv, prefix, factor, enter, reach, incoming)


def norm_kernel(parts, mixed_ref, gain_ref, out_hbm, rows, out, out_sem):
    heads, tokens, dim = mixed_ref.shape
    squares = [jnp.zeros((tokens, dim), F32) for _ in range(4)]
    for h in range(heads):
        x = mixed_ref[h].astype(F32)
        squares[h % 4] = squares[h % 4] + x * x
    total = squares[0] + squares[1] + squares[2] + squares[3]
    mean = jnp.sum(total, axis=1, keepdims=True) * (1.0 / (heads * dim))
    scale = jnp.broadcast_to(lax.rsqrt(mean + 1e-06), (tokens, dim))
    size = tokens // parts

    def copy_out(p):
        here = pl.ds(p * size, size)
        return pltpu.make_async_copy(out.at[here], out_hbm.at[here], out_sem.at[p])

    for p in range(parts):
        first, last = p * size, (p + 1) * size
        for h in range(heads):
            x = mixed_ref[h, first:last, :].astype(F32) * scale[first:last] * gain_ref[h : h + 1, :]
            rows[pl.ds(first * heads + h, size, stride=heads), :] = x
        for t in range(first, last):
            out[t] = rows[t * heads : (t + 1) * heads, :].astype(BF16)
        copy_out(p).start()
    for p in range(parts):
        copy_out(p).wait()


def norm(mixed, gain):
    heads, tokens, dim = mixed.shape
    parts = 6
    return pl.pallas_call(
        functools.partial(norm_kernel, parts),
        out_specs=pl.BlockSpec(memory_space=pl.ANY),
        out_shape=jax.ShapeDtypeStruct((tokens, heads, dim), BF16),
        scratch_shapes=[
            pltpu.VMEM((tokens * heads, dim), F32),
            pltpu.VMEM((tokens, heads, dim), BF16),
            pltpu.SemaphoreType.DMA((parts,)),
        ],
        compiler_params=pltpu.CompilerParams(vmem_limit_bytes=LIMIT),
        name="norm",
    )(mixed, gain)


def sent(pair):
    state, decay = pair
    high = lax.reduce_precision(decay, 8, 7)
    rows = [state, high, decay - high, jnp.zeros((6, state.shape[1]), F32)]
    return jnp.concatenate([row.astype(BF16) for row in rows], axis=0)


def received(rows):
    dim = rows.shape[1]
    rows = rows.astype(F32)
    return rows[:dim], rows[dim : dim + 1] + rows[dim + 1 : dim + 2]


def join(earlier, later):
    return later[1] * earlier[0] + later[0], earlier[1] * later[1]


def incoming_state(state, decay):
    segment = lax.axis_index("seg")
    count = lax.axis_size("seg")
    whole = (state, decay)
    entering = (jnp.zeros_like(state), jnp.ones_like(decay))
    hop = 1
    while hop < count // 2:
        other = received(lax.ppermute(sent(whole), "seg", [(i, i ^ hop) for i in range(count)]))
        upper = (segment & hop) != 0
        entering = jax.tree.map(lambda a, b: jnp.where(upper, a, b), join(other, entering), entering)
        whole = jax.tree.map(lambda a, b: jnp.where(upper, a, b), join(other, whole), join(whole, other))
        hop *= 2
    half = count // 2
    other = received(lax.ppermute(sent(whole), "seg", [(i, i + half) for i in range(half)]))
    return entering[1] * other[0] + entering[0]


def shards(queries, keys, values, decay_log, out_gain):
    per_block = lax.axis_size("head")
    group = ("sub", "head")
    kv = lax.all_to_all(pack_kv(keys, values, decay_log), group, 0, 0, tiled=True)
    query = lax.all_to_all(pack_q(queries, decay_log), group, 0, 0, tiled=True)
    prefix, total, decay, factor, enter, reach = states(kv, per_block)
    incoming = incoming_state(total, decay)
    mixed = attend(query, kv, prefix, factor, enter, reach, incoming)
    mixed = lax.all_to_all(mixed, group, 0, 0, tiled=True)
    return norm(mixed, out_gain)


def solution(mesh):
    devices = mesh.devices
    contexts, per_block = devices.shape
    heads = 64
    sub = heads // per_block
    split = Mesh(devices.reshape(contexts // sub, sub, per_block), ("seg", "sub", "head"))
    rows = ("seg", "sub", "head")
    return jax.shard_map(
        shards,
        mesh=split,
        in_specs=(P(rows, None, None), P(rows, None, None), P(rows, None, None), P(rows, None), P()),
        out_specs=P(rows, None, None),
        check_vma=False,
    )
```

profile of v0, /device:TPU:1, one launch (start us, length us, event | category | flops | bytes accessed | tf_op | source)
XLA Modules:
  0.0 129.5 jit_solution(8362613576015091983)
XLA Ops:
  0.0 4.0 %pack_kv.1 = bf16[64,104,128]{2,1,0:T(8,128)(2,1)} custom-call(bf16[48,64]{1,0:T(8,128)(2,1)} %decay_hbm.1, bf16[48,64,128]{2,1,0:T(8,128)(2,1)} %keys_hbm.1, bf16[48,64,128]{2,1,0:T(8,128)(2,1)} %values_hbm.1), custom_call_target="tpu_custom_call" | custom-call | tf_op jit(solution)/shard_map/pack_kv/pallas_call | solution.py:109
  4.0 11.6 %all-to-all-start.1 = ((bf16[64,104,128]{2,1,0:T(8,128)(2,1)}), bf16[64,104,128]{2,1,0:T(8,128)(2,1)S(1)}, u32[]{:S(2)}, u32[]{:S(2)}) async-start(bf16[64,104,128]{2,1,0:T(8,128)(2,1)} %pack_kv.1), calls=%async_computation.1 | async-start | bytes 3407872 | tf_op jit(solution)/shard_map/all_to_all | solution.py:371
  15.6 0.0 copy-start
  15.7 0.0 copy-start.1
  15.7 0.1 pad.11.clone
  15.8 41.9 %all-to-all-done.1.kv_ref = bf16[64,104,128]{2,1,0:T(8,128)(2,1)S(1)} async-done(((bf16[64,104,128]{2,1,0:T(8,128)(2,1)}), bf16[64,104,128]{2,1,0:T(8,128)(2,1)S(1)}, u32[]{:S(2)}, u32[]{:S(2)}) %all-to-all-start.1) | async-done | bytes 1703968 | tf_op jit(solution)/shard_map/all_to_all | solution.py:371
  57.7 0.7 states.1
  58.4 0.1 maximum_maximum_fusion
  58.5 4.0 %collective-permute-start = (bf16[136,128]{1,0:T(8,128)(2,1)S(1)}, bf16[136,128]{1,0:T(8,128)(2,1)S(1)}, u32[]{:S(2)}, u32[]{:S(2)}) collective-permute-start(bf16[136,128]{1,0:T(8,128)(2,1)S(1)} %maximum_maximum_fusion), channel_id=1, source_target_pairs={{0,64},{64,0},{128,192},{192,128},{256,320},{320,256},{384,448},{4... | collective-permute-start | bytes 104456 | tf_op jit(solution)/shard_map/ppermute | solution.py:358
  62.5 0.0 copy-done
  62.5 0.0 copy-done.1
  62.5 4.4 %pack_q.1 = bf16[64,48,128]{2,1,0:T(8,128)(2,1)} custom-call(bf16[48,64]{1,0:T(8,128)(2,1)S(1)} %copy-done.1, bf16[48,64,128]{2,1,0:T(8,128)(2,1)S(1)} %copy-done), custom_call_target="tpu_custom_call" | custom-call | tf_op jit(solution)/shard_map/pack_q/pallas_call | solution.py:145
  66.9 7.2 %all-to-all-start = ((bf16[64,48,128]{2,1,0:T(8,128)(2,1)}), bf16[64,48,128]{2,1,0:T(8,128)(2,1)S(1)}, u32[]{:S(2)}, u32[]{:S(2)}) async-start(bf16[64,48,128]{2,1,0:T(8,128)(2,1)} %pack_q.1), calls=%async_computation | async-start | bytes 1572864 | tf_op jit(solution)/shard_map/all_to_all | solution.py:372
  74.2 0.0 collective-permute-done
  74.3 0.1 maximum_maximum_fusion.1
  74.4 5.8 %collective-permute-start.1 = (bf16[136,128]{1,0:T(8,128)(2,1)S(1)}, bf16[136,128]{1,0:T(8,128)(2,1)S(1)}, u32[]{:S(2)}, u32[]{:S(2)}) collective-permute-start(bf16[136,128]{1,0:T(8,128)(2,1)S(1)} %maximum_maximum_fusion.1), channel_id=1, source_target_pairs={{0,128},{64,192},{128,0},{192,64},{256,384},{320,448},{384,256},{4... | collective-permute-start | bytes 104456 | tf_op jit(solution)/shard_map/ppermute | solution.py:358
  80.2 2.1 %collective-permute-done.1 = bf16[136,128]{1,0:T(8,128)(2,1)S(1)} collective-permute-done((bf16[136,128]{1,0:T(8,128)(2,1)S(1)}, bf16[136,128]{1,0:T(8,128)(2,1)S(1)}, u32[]{:S(2)}, u32[]{:S(2)}) %collective-permute-start.1) | collective-permute-done | bytes 34848 | tf_op jit(solution)/shard_map/ppermute | solution.py:358
  82.3 0.1 maximum_maximum_fusion.2
  82.4 8.1 %collective-permute-start.2 = (bf16[136,128]{1,0:T(8,128)(2,1)S(1)}, bf16[136,128]{1,0:T(8,128)(2,1)S(1)}, u32[]{:S(2)}, u32[]{:S(2)}) collective-permute-start(bf16[136,128]{1,0:T(8,128)(2,1)S(1)} %maximum_maximum_fusion.2), channel_id=1, source_target_pairs={{0,256},{64,320},{128,384},{192,448},{1,257},{65,321},{129,385},{1... | collective-permute-start | bytes 104456 | tf_op jit(solution)/shard_map/ppermute | solution.py:364
  90.5 1.0 collective-permute-done.2
  91.6 5.3 %all-to-all-done.query_ref = bf16[64,48,128]{2,1,0:T(8,128)(2,1)S(1)} async-done(((bf16[64,48,128]{2,1,0:T(8,128)(2,1)}), bf16[64,48,128]{2,1,0:T(8,128)(2,1)S(1)}, u32[]{:S(2)}, u32[]{:S(2)}) %all-to-all-start) | async-done | bytes 786464 | tf_op jit(solution)/shard_map/all_to_all | solution.py:372
  96.9 0.0 copy-start.2
  96.9 1.4 %attend.1 = bf16[64,48,128]{2,1,0:T(8,128)(2,1)S(1)} custom-call(bf16[64,48,128]{2,1,0:T(8,128)(2,1)S(1)} %all-to-all-done.query_ref, bf16[64,104,128]{2,1,0:T(8,128)(2,1)S(1)} %all-to-all-done.1.kv_ref, f32[8,128,128]{2,1,0:T(8,128)S(1)} %get-tuple-element.11.prefix_ref, f32[8,8,384]{2,1,0:T(8,128)S(1)} %get-tuple-element.12.factor_ref, ...), custom_call_target="tpu_custom_call" | custom-call | tf_op jit(solution)/shard_map/attend/pallas_call | solution.py:282
  98.3 29.2 %all_to_all.15.mixed_ref = bf16[64,48,128]{2,1,0:T(8,128)(2,1)S(1)} all-to-all(bf16[64,48,128]{2,1,0:T(8,128)(2,1)S(1)} %attend.1), channel_id=1, replica_groups=mesh['seg'=8,'sub'=8,'head'=8] {'sub','head'}, dimensions={0} | all-to-all | bytes 1572864 | tf_op jit(solution)/shard_map/all_to_all | solution.py:376
  127.5 0.0 copy-done.2
  127.5 2.0 %norm.1 = bf16[48,64,128]{2,1,0:T(8,128)(2,1)} custom-call(bf16[64,48,128]{2,1,0:T(8,128)(2,1)S(1)} %all_to_all.15.mixed_ref, f32[64,128]{1,0:T(8,128)S(1)} %copy-done.2), custom_call_target="tpu_custom_call" | custom-call | tf_op jit(solution)/shard_map/norm/pallas_call | solution.py:320
  (13 shorter events, 0.1 us)
Async XLA Ops:
  4.0 53.7 %all-to-all-start.1 = ((bf16[64,104,128]{2,1,0:T(8,128)(2,1)}), bf16[64,104,128]{2,1,0:T(8,128)(2,1)S(1)}, u32[]{:S(2)}, u32[]{:S(2)}) async-start(bf16[64,104,128]{2,1,0:T(8,128)(2,1)} %pack_kv.1), calls=%async_computation.1 | async-start | bytes 3407872 | tf_op jit(solution)/shard_map/all_to_all | solution.py:371
  15.6 46.9 %copy-start = (bf16[48,64,128]{2,1,0:T(8,128)(2,1)S(1)}, bf16[48,64,128]{2,1,0:T(8,128)(2,1)}, u32[]{:S(2)}) copy-start(bf16[48,64,128]{2,1,0:T(8,128)(2,1)} %queries_ref.1) | copy-start | bytes 2359300
  15.7 46.9 %copy-start.1 = (bf16[48,64]{1,0:T(8,128)(2,1)S(1)}, bf16[48,64]{1,0:T(8,128)(2,1)}, u32[]{:S(2)}) copy-start(bf16[48,64]{1,0:T(8,128)(2,1)} %decay_hbm.1) | copy-start | bytes 18436
  58.5 15.7 %collective-permute-start = (bf16[136,128]{1,0:T(8,128)(2,1)S(1)}, bf16[136,128]{1,0:T(8,128)(2,1)S(1)}, u32[]{:S(2)}, u32[]{:S(2)}) collective-permute-start(bf16[136,128]{1,0:T(8,128)(2,1)S(1)} %maximum_maximum_fusion), channel_id=1, source_target_pairs={{0,64},{64,0},{128,192},{192,128},{256,320},{320,256},{384,448},{4... | collective-permute-start | bytes 104456 | tf_op jit(solution)/shard_map/ppermute | solution.py:358
  66.9 30.0 %all-to-all-start = ((bf16[64,48,128]{2,1,0:T(8,128)(2,1)}), bf16[64,48,128]{2,1,0:T(8,128)(2,1)S(1)}, u32[]{:S(2)}, u32[]{:S(2)}) async-start(bf16[64,48,128]{2,1,0:T(8,128)(2,1)} %pack_q.1), calls=%async_computation | async-start | bytes 1572864 | tf_op jit(solution)/shard_map/all_to_all | solution.py:372
  74.4 7.9 %collective-permute-start.1 = (bf16[136,128]{1,0:T(8,128)(2,1)S(1)}, bf16[136,128]{1,0:T(8,128)(2,1)S(1)}, u32[]{:S(2)}, u32[]{:S(2)}) collective-permute-start(bf16[136,128]{1,0:T(8,128)(2,1)S(1)} %maximum_maximum_fusion.1), channel_id=1, source_target_pairs={{0,128},{64,192},{128,0},{192,64},{256,384},{320,448},{384,256},{4... | collective-permute-start | bytes 104456 | tf_op jit(solution)/shard_map/ppermute | solution.py:358
  82.4 9.1 %collective-permute-start.2 = (bf16[136,128]{1,0:T(8,128)(2,1)S(1)}, bf16[136,128]{1,0:T(8,128)(2,1)S(1)}, u32[]{:S(2)}, u32[]{:S(2)}) collective-permute-start(bf16[136,128]{1,0:T(8,128)(2,1)S(1)} %maximum_maximum_fusion.2), channel_id=1, source_target_pairs={{0,256},{64,320},{128,384},{192,448},{1,257},{65,321},{129,385},{1... | collective-permute-start | bytes 104456 | tf_op jit(solution)/shard_map/ppermute | solution.py:364
  96.9 30.6 %copy-start.2 = (f32[64,128]{1,0:T(8,128)S(1)}, f32[64,128]{1,0:T(8,128)}, u32[]{:S(2)}) copy-start(f32[64,128]{1,0:T(8,128)} %gain_ref.1) | copy-start | bytes 98308
where the time goes:
time: 130 us
  waiting for transfers between devices  50.4 us (39%)
  starting transfers between devices  36.7 us (28%)
  blocking collectives  29.2 us (22%)
  Pallas kernels  12.5 us (10%)
    all_to_all x1, waiting for transfers between devices, shards(): lax.all_to_all(pack_kv(keys, values, decay_log), group, 0, 0, tiled=True)  41.9 us
    all_to_all x1, blocking collectives, shards(): mixed = lax.all_to_all(mixed, group, 0, 0, tiled=True)  29.2 us
    all_to_all x1, starting transfers between devices, shards(): lax.all_to_all(pack_kv(keys, values, decay_log), group, 0, 0, tiled=True)  11.6 us
    ppermute x2, starting transfers between devices, incoming_state(): lax.ppermute(sent(whole), 'seg', [(i, i ^ hop) for i in range(count)])  9.81 us
    ppermute x1, starting transfers between devices, incoming_state(): lax.ppermute(sent(whole), 'seg', [(i, i + half) for i in range(half)])  8.07 us
    all_to_all x1, starting transfers between devices, shards(): query = lax.all_to_all(pack_q(queries, decay_log), group, 0, 0, tiled=True)  7.23 us
    all_to_all x1, waiting for transfers between devices, shards(): query = lax.all_to_all(pack_q(queries, decay_log), group, 0, 0, tiled=True)  5.35 us
    pallas_call x1, Pallas kernels, pack_q(): pl.pallas_call(pack_q_kernel, grid=(heads // 8,), in_specs=[pl.BlockSpec(...  4.4 us
  transfers between devices with their start and end apart: 5, of which 4 were waited for; matrix products, arithmetic and copies ran while one was open for 0% of the time, Pallas kernels for 3%

commit v1 on v0

--- a/solution.py
+++ b/solution.py
@@ -157,7 +157,7 @@
     )(decay, queries)
 
 
-def states_kernel(per_block, kv_ref, prefix_ref, total_ref, decay_ref, factor_ref, enter_ref, reach_ref):
+def states_kernel(per_block, kv_ref, prefix_ref, total_ref, factor_ref, enter_ref, reach_ref):
     sources, rows, dim = kv_ref.shape
     tokens = (rows - EXTRA) // 2
     blocks = sources // per_block
@@ -202,8 +202,10 @@
             preferred_element_type=F32,
         )
         state = jnp.exp(block_total[b : b + 1, :]) * state + own
-    total_ref[...] = state
-    decay_ref[...] = jnp.exp(jnp.sum(block_total, axis=0, keepdims=True))
+    total_ref[0:dim, :] = state
+    total_ref[dim : dim + 8, :] = jnp.broadcast_to(
+        jnp.sum(block_total, axis=0, keepdims=True), (8, dim)
+    )
 
 
 def states(kv, per_block):
@@ -213,8 +215,7 @@
         functools.partial(states_kernel, per_block),
         out_shape=(
             jax.ShapeDtypeStruct((blocks, dim, dim), F32),
-            jax.ShapeDtypeStruct((dim, dim), F32),
-            jax.ShapeDtypeStruct((1, dim), F32),
+            jax.ShapeDtypeStruct((dim + 8, dim), F32),
             jax.ShapeDtypeStruct((blocks, per_block, length), F32),
             jax.ShapeDtypeStruct((sources, dim), F32),
             jax.ShapeDtypeStruct((blocks, dim), F32),
@@ -331,47 +332,37 @@
     )(mixed, gain)
 
 
-def sent(pair):
-    state, decay = pair
-    high = lax.reduce_precision(decay, 8, 7)
-    rows = [state, high, decay - high, jnp.zeros((6, state.shape[1]), F32)]
-    return jnp.concatenate([row.astype(BF16) for row in rows], axis=0)
-
-
-def received(rows):
-    dim = rows.shape[1]
-    rows = rows.astype(F32)
-    return rows[:dim], rows[dim : dim + 1] + rows[dim + 1 : dim + 2]
-
-
-def join(earlier, later):
-    return later[1] * earlier[0] + later[0], earlier[1] * later[1]
-
-
-def incoming_state(state, decay):
+def incoming_state(own):
+    dim = own.shape[1]
     segment = lax.axis_index("seg")
     count = lax.axis_size("seg")
-    whole = (state, decay)
-    entering = (jnp.zeros_like(state), jnp.ones_like(decay))
+    whole = own
+    entering = jnp.zeros_like(own)
+
+    def join(earlier, later):
+        decay = jnp.exp(later[dim : dim + 1])
+        return jnp.concatenate([decay * earlier[:dim] + later[:dim], earlier[dim:] + later[dim:]], axis=0)
+
     hop = 1
     while hop < count // 2:
-        other = received(lax.ppermute(sent(whole), "seg", [(i, i ^ hop) for i in range(count)]))
+        other = lax.ppermute(whole, "seg", [(i, i ^ hop) for i in range(count)])
         upper = (segment & hop) != 0
-        entering = jax.tree.map(lambda a, b: jnp.where(upper, a, b), join(other, entering), entering)
-        whole = jax.tree.map(lambda a, b: jnp.where(upper, a, b), join(other, whole), join(whole, other))
+        entering = jnp.where(upper, join(other, entering), entering)
+        whole = jnp.where(upper, join(other, whole), join(whole, other))
         hop *= 2
     half = count // 2
-    other = received(lax.ppermute(sent(whole), "seg", [(i, i + half) for i in range(half)]))
-    return entering[1] * other[0] + entering[0]
+    other = lax.ppermute(whole, "seg", [(i, i + half) for i in range(half)])
+    return jnp.exp(entering[dim : dim + 1]) * other[:dim] + entering[:dim]
 
 
 def shards(queries, keys, values, decay_log, out_gain):
     per_block = lax.axis_size("head")
     group = ("sub", "head")
     kv = lax.all_to_all(pack_kv(keys, values, decay_log), group, 0, 0, tiled=True)
-    query = lax.all_to_all(pack_q(queries, decay_log), group, 0, 0, tiled=True)
-    prefix, total, decay, factor, enter, reach = states(kv, per_block)
-    incoming = incoming_state(total, decay)
+    query = pack_q(queries, decay_log)
+    query = lax.all_to_all(query, group, 0, 0, tiled=True)
+    prefix, total, factor, enter, reach = states(kv, per_block)
+    incoming = incoming_state(total)
     mixed = attend(query, kv, prefix, factor, enter, reach, incoming)
     mixed = lax.all_to_all(mixed, group, 0, 0, tiled=True)
     return norm(mixed, out_gain)

time: 130 us -> 128 us (0.985)
  waiting for transfers between devices: 50.4 us -> 43 us
  blocking collectives: 29.2 us -> 35.4 us
    all_to_all x1, blocking collectives: 29.2 us -> 35.4 us  [shards(): mixed = lax.all_to_all(mixed, group, 0, 0, tiled=True)]
    all_to_all x1, waiting for transfers between devices: 5.35 us -> 0.01 us  [shards(): query = lax.all_to_all(query, group, 0, 0, tiled=True)]
    all_to_all x1, waiting for transfers between devices: 41.9 us -> 37.6 us  [shards(): lax.all_to_all(pack_kv(keys, values, decay_log), group, 0, 0, tiled=True)]
    ppermute x3, waiting for transfers between devices: 3.11 us -> 5.4 us  [the longest x2 4.08 us: incoming_state(): other = lax.ppermute(whole, 'seg', [(i, i ^ hop) for i in range(count)])]
  transfers between devices with their start and end apart: 5 -> 5, of which waited for: 4 -> 4; matrix products, arithmetic and copies ran while one was open for 0% -> 0% of each run, Pallas kernels for 3% -> 4%
where the time goes in v1:
time: 128 us
  waiting for transfers between devices  43 us (34%)
  starting transfers between devices  36.8 us (29%)
  blocking collectives  35.4 us (28%)
  Pallas kernels  12.5 us (10%)
    all_to_all x1, waiting for transfers between devices, shards(): lax.all_to_all(pack_kv(keys, values, decay_log), group, 0, 0, tiled=True)  37.6 us
    all_to_all x1, blocking collectives, shards(): mixed = lax.all_to_all(mixed, group, 0, 0, tiled=True)  35.4 us
    all_to_all x1, starting transfers between devices, shards(): lax.all_to_all(pack_kv(keys, values, decay_log), group, 0, 0, tiled=True)  11.8 us
    ppermute x2, starting transfers between devices, incoming_state(): other = lax.ppermute(whole, 'seg', [(i, i ^ hop) for i in range(count)])  9.81 us
    ppermute x1, starting transfers between devices, incoming_state(): other = lax.ppermute(whole, 'seg', [(i, i + half) for i in range(half)])  8.28 us
    all_to_all x1, starting transfers between devices, shards(): query = lax.all_to_all(query, group, 0, 0, tiled=True)  6.95 us
    pallas_call x1, Pallas kernels, pack_q(): pl.pallas_call(pack_q_kernel, grid=(heads // 8,), in_specs=[pl.BlockSpec(...  4.4 us
    ppermute x2, waiting for transfers between devices, incoming_state(): other = lax.ppermute(whole, 'seg', [(i, i ^ hop) for i in range(count)])  4.08 us
  transfers between devices with their start and end apart: 5, of which 4 were waited for; matrix products, arithmetic and copies ran while one was open for 0% of the time, Pallas kernels for 4%

profile of v1, /device:TPU:1, one launch (start us, length us, event | category | flops | bytes accessed | tf_op | source)
XLA Modules:
  0.0 128.0 jit_solution(11798951269649983718)
XLA Ops:
  0.0 4.0 %pack_kv.1 = bf16[64,104,128]{2,1,0:T(8,128)(2,1)} custom-call(bf16[48,64]{1,0:T(8,128)(2,1)} %decay_hbm.1, bf16[48,64,128]{2,1,0:T(8,128)(2,1)} %keys_hbm.1, bf16[48,64,128]{2,1,0:T(8,128)(2,1)} %values_hbm.1), custom_call_target="tpu_custom_call" | custom-call | tf_op jit(solution)/shard_map/pack_kv/pallas_call | solution.py:109
  4.0 0.0 copy-start
  4.0 0.0 copy-start.1
  4.0 11.8 %all-to-all-start.1 = ((bf16[64,104,128]{2,1,0:T(8,128)(2,1)}), bf16[64,104,128]{2,1,0:T(8,128)(2,1)S(1)}, u32[]{:S(2)}, u32[]{:S(2)}) async-start(bf16[64,104,128]{2,1,0:T(8,128)(2,1)} %pack_kv.1), calls=%async_computation.1 | async-start | bytes 3407872 | tf_op jit(solution)/shard_map/all_to_all | solution.py:361
  15.8 0.0 copy-done
  15.8 0.0 copy-done.1
  15.8 4.4 %pack_q.1 = bf16[64,48,128]{2,1,0:T(8,128)(2,1)} custom-call(bf16[48,64]{1,0:T(8,128)(2,1)S(1)} %copy-done.1, bf16[48,64,128]{2,1,0:T(8,128)(2,1)S(1)} %copy-done), custom_call_target="tpu_custom_call" | custom-call | tf_op jit(solution)/shard_map/pack_q/pallas_call | solution.py:145
  20.2 37.6 %all-to-all-done.1.kv_ref = bf16[64,104,128]{2,1,0:T(8,128)(2,1)S(1)} async-done(((bf16[64,104,128]{2,1,0:T(8,128)(2,1)}), bf16[64,104,128]{2,1,0:T(8,128)(2,1)S(1)}, u32[]{:S(2)}, u32[]{:S(2)}) %all-to-all-start.1) | async-done | bytes 1703968 | tf_op jit(solution)/shard_map/all_to_all | solution.py:361
  57.8 6.9 %all-to-all-start = ((bf16[64,48,128]{2,1,0:T(8,128)(2,1)}), bf16[64,48,128]{2,1,0:T(8,128)(2,1)S(1)}, u32[]{:S(2)}, u32[]{:S(2)}) async-start(bf16[64,48,128]{2,1,0:T(8,128)(2,1)} %pack_q.1), calls=%async_computation | async-start | bytes 1572864 | tf_op jit(solution)/shard_map/all_to_all | solution.py:363
  64.8 0.7 states.1
  65.5 4.0 %collective-permute-start = (f32[136,128]{1,0:T(8,128)S(1)}, f32[136,128]{1,0:T(8,128)S(1)}, u32[]{:S(2)}, u32[]{:S(2)}) collective-permute-start(f32[136,128]{1,0:T(8,128)S(1)} %get-tuple-element.14), channel_id=1, source_target_pairs={{0,64},{64,0},{128,192},{192,128},{256,320},{320,256},{384,448},{4... | collective-permute-start | bytes 208904 | tf_op jit(solution)/shard_map/ppermute | solution.py:348
  69.5 2.1 %collective-permute-done = f32[136,128]{1,0:T(8,128)S(1)} collective-permute-done((f32[136,128]{1,0:T(8,128)S(1)}, f32[136,128]{1,0:T(8,128)S(1)}, u32[]{:S(2)}, u32[]{:S(2)}) %collective-permute-start) | collective-permute-done | bytes 69664 | tf_op jit(solution)/shard_map/ppermute | solution.py:348
  71.7 5.8 %collective-permute-start.1 = (f32[136,128]{1,0:T(8,128)S(1)}, f32[136,128]{1,0:T(8,128)S(1)}, u32[]{:S(2)}, u32[]{:S(2)}) collective-permute-start(f32[136,128]{1,0:T(8,128)S(1)} %fusion.1), channel_id=1, source_target_pairs={{0,128},{64,192},{128,0},{192,64},{256,384},{320,448},{384,256},{4... | collective-permute-start | bytes 208904 | tf_op jit(solution)/shard_map/ppermute | solution.py:348
  77.6 1.9 %collective-permute-done.1 = f32[136,128]{1,0:T(8,128)S(1)} collective-permute-done((f32[136,128]{1,0:T(8,128)S(1)}, f32[136,128]{1,0:T(8,128)S(1)}, u32[]{:S(2)}, u32[]{:S(2)}) %collective-permute-start.1) | collective-permute-done | bytes 69664 | tf_op jit(solution)/shard_map/ppermute | solution.py:348
  79.6 8.3 %collective-permute-start.2 = (f32[136,128]{1,0:T(8,128)S(1)}, f32[136,128]{1,0:T(8,128)S(1)}, u32[]{:S(2)}, u32[]{:S(2)}) collective-permute-start(f32[136,128]{1,0:T(8,128)S(1)} %fusion), channel_id=1, source_target_pairs={{0,256},{64,320},{128,384},{192,448},{1,257},{65,321},{129,385},{1... | collective-permute-start | bytes 208904 | tf_op jit(solution)/shard_map/ppermute | solution.py:354
  87.9 1.3 %collective-permute-done.2 = f32[136,128]{1,0:T(8,128)S(1)} collective-permute-done((f32[136,128]{1,0:T(8,128)S(1)}, f32[136,128]{1,0:T(8,128)S(1)}, u32[]{:S(2)}, u32[]{:S(2)}) %collective-permute-start.2) | collective-permute-done | bytes 69664 | tf_op jit(solution)/shard_map/ppermute | solution.py:354
  89.2 0.0 all-to-all-done.query_ref
  89.2 0.0 copy-start.2
  89.2 1.4 %attend.1 = bf16[64,48,128]{2,1,0:T(8,128)(2,1)S(1)} custom-call(bf16[64,48,128]{2,1,0:T(8,128)(2,1)S(1)} %all-to-all-done.query_ref, bf16[64,104,128]{2,1,0:T(8,128)(2,1)S(1)} %all-to-all-done.1.kv_ref, f32[8,128,128]{2,1,0:T(8,128)S(1)} %get-tuple-element.10.prefix_ref, f32[8,8,384]{2,1,0:T(8,128)S(1)} %get-tuple-element.11.factor_ref, ...), custom_call_target="tpu_custom_call" | custom-call | tf_op jit(solution)/shard_map/attend/pallas_call | solution.py:283
  90.7 35.4 %all_to_all.15.mixed_ref = bf16[64,48,128]{2,1,0:T(8,128)(2,1)S(1)} all-to-all(bf16[64,48,128]{2,1,0:T(8,128)(2,1)S(1)} %attend.1), channel_id=1, replica_groups=mesh['seg'=8,'sub'=8,'head'=8] {'sub','head'}, dimensions={0} | all-to-all | bytes 1572864 | tf_op jit(solution)/shard_map/all_to_all | solution.py:367
  126.0 0.0 copy-done.2
  126.0 2.0 %norm.1 = bf16[48,64,128]{2,1,0:T(8,128)(2,1)} custom-call(bf16[64,48,128]{2,1,0:T(8,128)(2,1)S(1)} %all_to_all.15.mixed_ref, f32[64,128]{1,0:T(8,128)S(1)} %copy-done.2), custom_call_target="tpu_custom_call" | custom-call | tf_op jit(solution)/shard_map/norm/pallas_call | solution.py:321
  (14 shorter events, 0.1 us)
Async XLA Ops:
  4.0 11.8 %copy-start = (bf16[48,64,128]{2,1,0:T(8,128)(2,1)S(1)}, bf16[48,64,128]{2,1,0:T(8,128)(2,1)}, u32[]{:S(2)}) copy-start(bf16[48,64,128]{2,1,0:T(8,128)(2,1)} %queries_ref.1) | copy-start | bytes 2359300
  4.0 11.8 %copy-start.1 = (bf16[48,64]{1,0:T(8,128)(2,1)S(1)}, bf16[48,64]{1,0:T(8,128)(2,1)}, u32[]{:S(2)}) copy-start(bf16[48,64]{1,0:T(8,128)(2,1)} %decay_hbm.1) | copy-start | bytes 18436
  4.0 53.8 %all-to-all-start.1 = ((bf16[64,104,128]{2,1,0:T(8,128)(2,1)}), bf16[64,104,128]{2,1,0:T(8,128)(2,1)S(1)}, u32[]{:S(2)}, u32[]{:S(2)}) async-start(bf16[64,104,128]{2,1,0:T(8,128)(2,1)} %pack_kv.1), calls=%async_computation.1 | async-start | bytes 3407872 | tf_op jit(solution)/shard_map/all_to_all | solution.py:361
  57.8 31.4 %all-to-all-start = ((bf16[64,48,128]{2,1,0:T(8,128)(2,1)}), bf16[64,48,128]{2,1,0:T(8,128)(2,1)S(1)}, u32[]{:S(2)}, u32[]{:S(2)}) async-start(bf16[64,48,128]{2,1,0:T(8,128)(2,1)} %pack_q.1), calls=%async_computation | async-start | bytes 1572864 | tf_op jit(solution)/shard_map/all_to_all | solution.py:363
  65.5 6.2 %collective-permute-start = (f32[136,128]{1,0:T(8,128)S(1)}, f32[136,128]{1,0:T(8,128)S(1)}, u32[]{:S(2)}, u32[]{:S(2)}) collective-permute-start(f32[136,128]{1,0:T(8,128)S(1)} %get-tuple-element.14), channel_id=1, source_target_pairs={{0,64},{64,0},{128,192},{192,128},{256,320},{320,256},{384,448},{4... | collective-permute-start | bytes 208904 | tf_op jit(solution)/shard_map/ppermute | solution.py:348
  71.7 7.8 %collective-permute-start.1 = (f32[136,128]{1,0:T(8,128)S(1)}, f32[136,128]{1,0:T(8,128)S(1)}, u32[]{:S(2)}, u32[]{:S(2)}) collective-permute-start(f32[136,128]{1,0:T(8,128)S(1)} %fusion.1), channel_id=1, source_target_pairs={{0,128},{64,192},{128,0},{192,64},{256,384},{320,448},{384,256},{4... | collective-permute-start | bytes 208904 | tf_op jit(solution)/shard_map/ppermute | solution.py:348
  79.6 9.6 %collective-permute-start.2 = (f32[136,128]{1,0:T(8,128)S(1)}, f32[136,128]{1,0:T(8,128)S(1)}, u32[]{:S(2)}, u32[]{:S(2)}) collective-permute-start(f32[136,128]{1,0:T(8,128)S(1)} %fusion), channel_id=1, source_target_pairs={{0,256},{64,320},{128,384},{192,448},{1,257},{65,321},{129,385},{1... | collective-permute-start | bytes 208904 | tf_op jit(solution)/shard_map/ppermute | solution.py:354
  89.2 36.8 %copy-start.2 = (f32[64,128]{1,0:T(8,128)S(1)}, f32[64,128]{1,0:T(8,128)}, u32[]{:S(2)}) copy-start(f32[64,128]{1,0:T(8,128)} %gain_ref.1) | copy-start | bytes 98308

commit v2 on v1

--- a/solution.py
+++ b/solution.py
@@ -203,9 +203,8 @@
         )
         state = jnp.exp(block_total[b : b + 1, :]) * state + own
     total_ref[0:dim, :] = state
-    total_ref[dim : dim + 8, :] = jnp.broadcast_to(
-        jnp.sum(block_total, axis=0, keepdims=True), (8, dim)
-    )
+    decay = jnp.exp(jnp.sum(block_total, axis=0, keepdims=True))
+    total_ref[dim : dim + EXTRA, :] = jnp.broadcast_to(decay, (EXTRA, dim))
 
 
 def states(kv, per_block):
@@ -215,7 +214,7 @@
         functools.partial(states_kernel, per_block),
         out_shape=(
             jax.ShapeDtypeStruct((blocks, dim, dim), F32),
-            jax.ShapeDtypeStruct((dim + 8, dim), F32),
+            jax.ShapeDtypeStruct((dim + EXTRA, dim), F32),
             jax.ShapeDtypeStruct((blocks, per_block, length), F32),
             jax.ShapeDtypeStruct((sources, dim), F32),
             jax.ShapeDtypeStruct((blocks, dim), F32),
@@ -332,27 +331,33 @@
     )(mixed, gain)
 
 
+def received(rows):
+    dim = rows.shape[1]
+    rows = rows.astype(F32)
+    return rows[:dim], rows[dim : dim + 1]
+
+
 def incoming_state(own):
     dim = own.shape[1]
     segment = lax.axis_index("seg")
     count = lax.axis_size("seg")
     whole = own
-    entering = jnp.zeros_like(own)
-
-    def join(earlier, later):
-        decay = jnp.exp(later[dim : dim + 1])
-        return jnp.concatenate([decay * earlier[:dim] + later[:dim], earlier[dim:] + later[dim:]], axis=0)
-
+    entering_state, entering_decay = jnp.zeros((dim, dim), F32), jnp.ones((1, dim), F32)
     hop = 1
     while hop < count // 2:
-        other = lax.ppermute(whole, "seg", [(i, i ^ hop) for i in range(count)])
-        upper = (segment & hop) != 0
-        entering = jnp.where(upper, join(other, entering), entering)
-        whole = jnp.where(upper, join(other, whole), join(whole, other))
+        mine = whole.astype(BF16)
+        state, decay = received(lax.ppermute(mine, "seg", [(i, i ^ hop) for i in range(count)]))
+        upper = ((segment & hop) != 0).astype(F32)
+        lower = 1.0 - upper
+        entering_state = (upper * entering_decay) * state + entering_state
+        entering_decay = entering_decay * (upper * decay + lower)
+        own_decay = whole[dim : dim + 1]
+        joined = (upper * own_decay + lower) * state + (lower * decay + upper) * whole[:dim]
+        whole = jnp.concatenate([joined, jnp.broadcast_to(decay * own_decay, (EXTRA, dim))], axis=0)
         hop *= 2
     half = count // 2
-    other = lax.ppermute(whole, "seg", [(i, i + half) for i in range(half)])
-    return jnp.exp(entering[dim : dim + 1]) * other[:dim] + entering[:dim]
+    state, _ = received(lax.ppermute(whole.astype(BF16), "seg", [(i, i + half) for i in range(half)]))
+    return entering_decay * state + entering_state
 
 
 def shards(queries, keys, values, decay_log, out_gain):

time: 128 us -> 127 us (level)
  no operation moved by 1% of the time
where the time goes in v2:
time: 127 us
  waiting for transfers between devices  41.8 us (33%)
  starting transfers between devices  37 us (29%)
  blocking collectives  35.4 us (28%)
  Pallas kernels  12.5 us (10%)
    all_to_all x1, waiting for transfers between devices, shards(): lax.all_to_all(pack_kv(keys, values, decay_log), group, 0, 0, tiled=True)  37.6 us
    all_to_all x1, blocking collectives, shards(): mixed = lax.all_to_all(mixed, group, 0, 0, tiled=True)  35.4 us
    all_to_all x1, starting transfers between devices, shards(): lax.all_to_all(pack_kv(keys, values, decay_log), group, 0, 0, tiled=True)  11.8 us
    ppermute x2, starting transfers between devices, incoming_state(): lax.ppermute(mine, 'seg', [(i, i ^ hop) for i in range(count)])  9.81 us
    ppermute x1, starting transfers between devices, incoming_state(): lax.ppermute(whole.astype(BF16), 'seg', [(i, i + half) for i in range(hal...  8.45 us
    all_to_all x1, starting transfers between devices, shards(): query = lax.all_to_all(query, group, 0, 0, tiled=True)  6.95 us
    pallas_call x1, Pallas kernels, pack_q(): pl.pallas_call(pack_q_kernel, grid=(heads // 8,), in_specs=[pl.BlockSpec(...  4.4 us
    pallas_call x1, Pallas kernels, pack_kv(): pl.pallas_call(pack_kv_kernel, in_specs=[anywhere] * 3, out_specs=anywher...  4.01 us
  transfers between devices with their start and end apart: 5, of which 4 were waited for; matrix products, arithmetic and copies ran while one was open for 0% of the time, Pallas kernels for 4%

profile of v2, /device:TPU:1, one launch (start us, length us, event | category | flops | bytes accessed | tf_op | source)
XLA Modules:
  0.0 127.0 jit_solution(12045522098835399185)
XLA Ops:
  0.0 4.0 %pack_kv.1 = bf16[64,104,128]{2,1,0:T(8,128)(2,1)} custom-call(bf16[48,64]{1,0:T(8,128)(2,1)} %decay_hbm.1, bf16[48,64,128]{2,1,0:T(8,128)(2,1)} %keys_hbm.1, bf16[48,64,128]{2,1,0:T(8,128)(2,1)} %values_hbm.1), custom_call_target="tpu_custom_call" | custom-call | tf_op jit(solution)/shard_map/pack_kv/pallas_call | solution.py:109
  4.0 0.0 copy-start
  4.0 0.0 copy-start.1
  4.0 11.8 %all-to-all-start.1 = ((bf16[64,104,128]{2,1,0:T(8,128)(2,1)}), bf16[64,104,128]{2,1,0:T(8,128)(2,1)S(1)}, u32[]{:S(2)}, u32[]{:S(2)}) async-start(bf16[64,104,128]{2,1,0:T(8,128)(2,1)} %pack_kv.1), calls=%async_computation.1 | async-start | bytes 3407872 | tf_op jit(solution)/shard_map/all_to_all | solution.py:366
  15.8 0.0 copy-done
  15.8 0.0 copy-done.1
  15.8 4.4 %pack_q.1 = bf16[64,48,128]{2,1,0:T(8,128)(2,1)} custom-call(bf16[48,64]{1,0:T(8,128)(2,1)S(1)} %copy-done.1, bf16[48,64,128]{2,1,0:T(8,128)(2,1)S(1)} %copy-done), custom_call_target="tpu_custom_call" | custom-call | tf_op jit(solution)/shard_map/pack_q/pallas_call | solution.py:145
  20.2 37.6 %all-to-all-done.1.kv_ref = bf16[64,104,128]{2,1,0:T(8,128)(2,1)S(1)} async-done(((bf16[64,104,128]{2,1,0:T(8,128)(2,1)}), bf16[64,104,128]{2,1,0:T(8,128)(2,1)S(1)}, u32[]{:S(2)}, u32[]{:S(2)}) %all-to-all-start.1) | async-done | bytes 1703968 | tf_op jit(solution)/shard_map/all_to_all | solution.py:366
  57.8 6.9 %all-to-all-start = ((bf16[64,48,128]{2,1,0:T(8,128)(2,1)}), bf16[64,48,128]{2,1,0:T(8,128)(2,1)S(1)}, u32[]{:S(2)}, u32[]{:S(2)}) async-start(bf16[64,48,128]{2,1,0:T(8,128)(2,1)} %pack_q.1), calls=%async_computation | async-start | bytes 1572864 | tf_op jit(solution)/shard_map/all_to_all | solution.py:368
  64.8 0.7 states.1
  65.5 4.0 %collective-permute-start = (bf16[136,128]{1,0:T(8,128)(2,1)S(1)}, bf16[136,128]{1,0:T(8,128)(2,1)S(1)}, u32[]{:S(2)}, u32[]{:S(2)}) collective-permute-start(bf16[136,128]{1,0:T(8,128)(2,1)S(1)} %convert_element_type.19), channel_id=1, source_target_pairs={{0,64},{64,0},{128,192},{192,128},{256,320},{320,256},{384,448},{4... | collective-permute-start | bytes 104456 | tf_op jit(solution)/shard_map/ppermute | solution.py:349
  69.6 1.6 %collective-permute-done = bf16[136,128]{1,0:T(8,128)(2,1)S(1)} collective-permute-done((bf16[136,128]{1,0:T(8,128)(2,1)S(1)}, bf16[136,128]{1,0:T(8,128)(2,1)S(1)}, u32[]{:S(2)}, u32[]{:S(2)}) %collective-permute-start) | collective-permute-done | bytes 34848 | tf_op jit(solution)/shard_map/ppermute | solution.py:349
  71.2 5.8 %collective-permute-start.1 = (bf16[136,128]{1,0:T(8,128)(2,1)S(1)}, bf16[136,128]{1,0:T(8,128)(2,1)S(1)}, u32[]{:S(2)}, u32[]{:S(2)}) collective-permute-start(bf16[136,128]{1,0:T(8,128)(2,1)S(1)} %pad_maximum_fusion), channel_id=1, source_target_pairs={{0,128},{64,192},{128,0},{192,64},{256,384},{320,448},{384,256},{4... | collective-permute-start | bytes 104456 | tf_op jit(solution)/shard_map/ppermute | solution.py:349
  77.0 1.6 %collective-permute-done.1 = bf16[136,128]{1,0:T(8,128)(2,1)S(1)} collective-permute-done((bf16[136,128]{1,0:T(8,128)(2,1)S(1)}, bf16[136,128]{1,0:T(8,128)(2,1)S(1)}, u32[]{:S(2)}, u32[]{:S(2)}) %collective-permute-start.1) | collective-permute-done | bytes 34848 | tf_op jit(solution)/shard_map/ppermute | solution.py:349
  78.7 8.4 %collective-permute-start.2 = (bf16[136,128]{1,0:T(8,128)(2,1)S(1)}, bf16[136,128]{1,0:T(8,128)(2,1)S(1)}, u32[]{:S(2)}, u32[]{:S(2)}) collective-permute-start(bf16[136,128]{1,0:T(8,128)(2,1)S(1)} %pad_maximum_fusion.1), channel_id=1, source_target_pairs={{0,256},{64,320},{128,384},{192,448},{1,257},{65,321},{129,385},{1... | collective-permute-start | bytes 104456 | tf_op jit(solution)/shard_map/ppermute | solution.py:359
  87.2 1.0 collective-permute-done.2
  88.2 0.0 all-to-all-done.query_ref
  88.2 0.0 copy-start.2
  88.2 1.4 %attend.1 = bf16[64,48,128]{2,1,0:T(8,128)(2,1)S(1)} custom-call(bf16[64,48,128]{2,1,0:T(8,128)(2,1)S(1)} %all-to-all-done.query_ref, bf16[64,104,128]{2,1,0:T(8,128)(2,1)S(1)} %all-to-all-done.1.kv_ref, f32[8,128,128]{2,1,0:T(8,128)S(1)} %get-tuple-element.10.prefix_ref, f32[8,8,384]{2,1,0:T(8,128)S(1)} %get-tuple-element.11.factor_ref, ...), custom_call_target="tpu_custom_call" | custom-call | tf_op jit(solution)/shard_map/attend/pallas_call | solution.py:282
  89.7 35.4 %all_to_all.15.mixed_ref = bf16[64,48,128]{2,1,0:T(8,128)(2,1)S(1)} all-to-all(bf16[64,48,128]{2,1,0:T(8,128)(2,1)S(1)} %attend.1), channel_id=1, replica_groups=mesh['seg'=8,'sub'=8,'head'=8] {'sub','head'}, dimensions={0} | all-to-all | bytes 1572864 | tf_op jit(solution)/shard_map/all_to_all | solution.py:372
  125.1 0.0 copy-done.2
  125.1 2.0 %norm.1 = bf16[48,64,128]{2,1,0:T(8,128)(2,1)} custom-call(bf16[64,48,128]{2,1,0:T(8,128)(2,1)S(1)} %all_to_all.15.mixed_ref, f32[64,128]{1,0:T(8,128)S(1)} %copy-done.2), custom_call_target="tpu_custom_call" | custom-call | tf_op jit(solution)/shard_map/norm/pallas_call | solution.py:320
  (12 shorter events, 0.1 us)
Async XLA Ops:
  4.0 11.8 %copy-start = (bf16[48,64,128]{2,1,0:T(8,128)(2,1)S(1)}, bf16[48,64,128]{2,1,0:T(8,128)(2,1)}, u32[]{:S(2)}) copy-start(bf16[48,64,128]{2,1,0:T(8,128)(2,1)} %queries_ref.1) | copy-start | bytes 2359300
  4.0 11.8 %copy-start.1 = (bf16[48,64]{1,0:T(8,128)(2,1)S(1)}, bf16[48,64]{1,0:T(8,128)(2,1)}, u32[]{:S(2)}) copy-start(bf16[48,64]{1,0:T(8,128)(2,1)} %decay_hbm.1) | copy-start | bytes 18436
  4.0 53.8 %all-to-all-start.1 = ((bf16[64,104,128]{2,1,0:T(8,128)(2,1)}), bf16[64,104,128]{2,1,0:T(8,128)(2,1)S(1)}, u32[]{:S(2)}, u32[]{:S(2)}) async-start(bf16[64,104,128]{2,1,0:T(8,128)(2,1)} %pack_kv.1), calls=%async_computation.1 | async-start | bytes 3407872 | tf_op jit(solution)/shard_map/all_to_all | solution.py:366
  57.8 30.4 %all-to-all-start = ((bf16[64,48,128]{2,1,0:T(8,128)(2,1)}), bf16[64,48,128]{2,1,0:T(8,128)(2,1)S(1)}, u32[]{:S(2)}, u32[]{:S(2)}) async-start(bf16[64,48,128]{2,1,0:T(8,128)(2,1)} %pack_q.1), calls=%async_computation | async-start | bytes 1572864 | tf_op jit(solution)/shard_map/all_to_all | solution.py:368
  65.5 5.6 %collective-permute-start = (bf16[136,128]{1,0:T(8,128)(2,1)S(1)}, bf16[136,128]{1,0:T(8,128)(2,1)S(1)}, u32[]{:S(2)}, u32[]{:S(2)}) collective-permute-start(bf16[136,128]{1,0:T(8,128)(2,1)S(1)} %convert_element_type.19), channel_id=1, source_target_pairs={{0,64},{64,0},{128,192},{192,128},{256,320},{320,256},{384,448},{4... | collective-permute-start | bytes 104456 | tf_op jit(solution)/shard_map/ppermute | solution.py:349
  71.2 7.4 %collective-permute-start.1 = (bf16[136,128]{1,0:T(8,128)(2,1)S(1)}, bf16[136,128]{1,0:T(8,128)(2,1)S(1)}, u32[]{:S(2)}, u32[]{:S(2)}) collective-permute-start(bf16[136,128]{1,0:T(8,128)(2,1)S(1)} %pad_maximum_fusion), channel_id=1, source_target_pairs={{0,128},{64,192},{128,0},{192,64},{256,384},{320,448},{384,256},{4... | collective-permute-start | bytes 104456 | tf_op jit(solution)/shard_map/ppermute | solution.py:349
  78.7 9.5 %collective-permute-start.2 = (bf16[136,128]{1,0:T(8,128)(2,1)S(1)}, bf16[136,128]{1,0:T(8,128)(2,1)S(1)}, u32[]{:S(2)}, u32[]{:S(2)}) collective-permute-start(bf16[136,128]{1,0:T(8,128)(2,1)S(1)} %pad_maximum_fusion.1), channel_id=1, source_target_pairs={{0,256},{64,320},{128,384},{192,448},{1,257},{65,321},{129,385},{1... | collective-permute-start | bytes 104456 | tf_op jit(solution)/shard_map/ppermute | solution.py:359
  88.2 36.8 %copy-start.2 = (f32[64,128]{1,0:T(8,128)S(1)}, f32[64,128]{1,0:T(8,128)}, u32[]{:S(2)}) copy-start(f32[64,128]{1,0:T(8,128)} %gain_ref.1) | copy-start | bytes 98308

commit v3 on v2

--- a/solution.py
+++ b/solution.py
@@ -157,6 +157,10 @@
     )(decay, queries)
 
 
+def block_of(ref, b, blocks, first, last):
+    return jnp.concatenate([ref[i, first:last, :] for i in range(b, ref.shape[0], blocks)], axis=0)
+
+
 def states_kernel(per_block, kv_ref, prefix_ref, total_ref, factor_ref, enter_ref, reach_ref):
     sources, rows, dim = kv_ref.shape
     tokens = (rows - EXTRA) // 2
@@ -166,23 +170,24 @@
     totals = jnp.sum(tail, axis=1)
     parts = three_parts(totals)
     at, of = iota((sources, sources), 0), iota((sources, sources), 1)
-    same = at // per_block == of // per_block
+    same = at // per_block == of % blocks
+    at_place, of_place = at % per_block, of // blocks
 
     def mask(keep):
         return keep.astype(F32).astype(BF16)
 
-    before = dot_parts(mask(same & (of < at)), parts)
-    after = dot_parts(mask(same & (of > at)), parts)
+    before = dot_parts(mask(same & (of_place < at_place)), parts)
+    after = dot_parts(mask(same & (of_place > at_place)), parts)
     enter_ref[...] = jnp.exp(before)
     to_block_end = jnp.exp(after)
-    block_at, source_of = iota((blocks, sources), 0), iota((blocks, sources), 1) // per_block
+    block_at, source_of = iota((blocks, sources), 0), iota((blocks, sources), 1) % blocks
     block_total = dot_parts(mask(block_at == source_of), parts)
     block_before = dot_parts(mask(block_at > source_of), parts)
     reach_ref[...] = jnp.exp(block_before)
     in_lanes = jnp.transpose(totals)[0:blocks, :]
     picked = jnp.where(block_at == source_of, in_lanes, 0.0)
     member, position = iota((sources, length), 0), iota((sources, length), 1)
-    up_to = mask(lax.rem(member, per_block) <= position // tokens)
+    up_to = mask(member // blocks <= position // tokens)
     through = sum(jnp.dot(part, up_to, preferred_element_type=F32) for part in three_parts(picked))
     source_row = iota((per_block, length), 0)
     source_col = iota((per_block, length), 1) // tokens
@@ -195,10 +200,15 @@
             source_col <= source_row, jnp.exp(start - through[b : b + 1, :]), 0.0
         )
         prefix_ref[b] = state
-        keys = kv_ref[here, 0:tokens, :].astype(F32) * to_block_end[here][:, None, :]
-        values = kv_ref[here, tokens : 2 * tokens, :].reshape(length, dim)
+        keys = jnp.concatenate(
+            [
+                kv_ref[p * blocks + b, 0:tokens, :].astype(F32) * to_block_end[b * per_block + p][None]
+                for p in range(per_block)
+            ],
+            axis=0,
+        )
         own = lax.dot_general(
-            keys.astype(BF16).reshape(length, dim), values, (((0,), (0,)), ((), ())),
+            keys.astype(BF16), block_of(kv_ref, b, blocks, tokens, 2 * tokens), (((0,), (0,)), ((), ())),
             preferred_element_type=F32,
         )
         state = jnp.exp(block_total[b : b + 1, :]) * state + own
@@ -238,9 +248,8 @@
         )
 
     def weights(b):
-        here = slice(b * per_block, (b + 1) * per_block)
-        query = query_ref[here].reshape(length, dim)
-        key = kv_ref[here, 0:tokens, :].reshape(length, dim)
+        query = block_of(query_ref, b, blocks, 0, tokens)
+        key = block_of(kv_ref, b, blocks, 0, tokens)
         factor = spread(factor_ref[b])
         tiles = []
         for low in range(0, length, step):
@@ -257,8 +266,8 @@
 
     def finish(b, tiles):
         here = slice(b * per_block, (b + 1) * per_block)
-        query = query_ref[here].reshape(length, dim)
-        value = kv_ref[here, tokens : 2 * tokens, :].reshape(length, dim)
+        query = block_of(query_ref, b, blocks, 0, tokens)
+        value = block_of(kv_ref, b, blocks, tokens, 2 * tokens)
         state = prefix_ref[b] + reach_ref[b : b + 1, :] * incoming_ref[...]
         inter = jnp.dot(query, state.astype(BF16), preferred_element_type=F32)
         enter = spread(enter_ref[here])
@@ -269,7 +278,7 @@
             for i in range(low // 16, high // 16):
                 source, row = divmod(i * 16, tokens)
                 piece = mixed[i * 16 - low : i * 16 - low + 16]
-                out_ref[b * per_block + source, row : row + 16, :] = piece
+                out_ref[source * blocks + b, row : row + 16, :] = piece
 
     tiles = weights(0)
     for b in range(blocks):
@@ -356,13 +365,15 @@
         whole = jnp.concatenate([joined, jnp.broadcast_to(decay * own_decay, (EXTRA, dim))], axis=0)
         hop *= 2
     half = count // 2
-    state, _ = received(lax.ppermute(whole.astype(BF16), "seg", [(i, i + half) for i in range(half)]))
+    state, _ = received(lax.ppermute(
+        whole.astype(BF16), "seg", [(i, half + (i + half // 2) % half) for i in range(half)]
+    ))
     return entering_decay * state + entering_state
 
 
 def shards(queries, keys, values, decay_log, out_gain):
     per_block = lax.axis_size("head")
-    group = ("sub", "head")
+    group = ("head", "sub")
     kv = lax.all_to_all(pack_kv(keys, values, decay_log), group, 0, 0, tiled=True)
     query = pack_q(queries, decay_log)
     query = lax.all_to_all(query, group, 0, 0, tiled=True)

time: 127 us -> 127 us (level)
  no operation moved by 1% of the time
where the time goes in v3:
time: 127 us; the launch traced here: 126 us
  waiting for transfers between devices  41.4 us (33%)
  starting transfers between devices  36.7 us (29%)
  blocking collectives  35.5 us (28%)
  Pallas kernels  12.5 us (10%)
    all_to_all x1, waiting for transfers between devices, shards(): lax.all_to_all(pack_kv(keys, values, decay_log), group, 0, 0, tiled=True)  37.2 us
    all_to_all x1, blocking collectives, shards(): mixed = lax.all_to_all(mixed, group, 0, 0, tiled=True)  35.5 us
    all_to_all x1, starting transfers between devices, shards(): lax.all_to_all(pack_kv(keys, values, decay_log), group, 0, 0, tiled=True)  11.8 us
    ppermute x2, starting transfers between devices, incoming_state(): lax.ppermute(mine, 'seg', [(i, i ^ hop) for i in range(count)])  9.81 us
    ppermute x1, starting transfers between devices, incoming_state(): lax.ppermute(whole.astype(BF16), 'seg', [(i, half + (i + half // 2) % hal...  8.47 us
    all_to_all x1, starting transfers between devices, shards(): query = lax.all_to_all(query, group, 0, 0, tiled=True)  6.65 us
    pallas_call x1, Pallas kernels, pack_q(): pl.pallas_call(pack_q_kernel, grid=(heads // 8,), in_specs=[pl.BlockSpec(...  4.4 us
    pallas_call x1, Pallas kernels, pack_kv(): pl.pallas_call(pack_kv_kernel, in_specs=[anywhere] * 3, out_specs=anywher...  4.01 us
  transfers between devices with their start and end apart: 5, of which 4 were waited for; matrix products, arithmetic and copies ran while one was open for 0% of the time, Pallas kernels for 4%

profile of v3, /device:TPU:1, one launch (start us, length us, event | category | flops | bytes accessed | tf_op | source)
XLA Modules:
  0.0 126.4 jit_solution(18296001678163832945)
XLA Ops:
  0.0 4.0 %pack_kv.1 = bf16[64,104,128]{2,1,0:T(8,128)(2,1)} custom-call(bf16[48,64]{1,0:T(8,128)(2,1)} %decay_hbm.1, bf16[48,64,128]{2,1,0:T(8,128)(2,1)} %keys_hbm.1, bf16[48,64,128]{2,1,0:T(8,128)(2,1)} %values_hbm.1), custom_call_target="tpu_custom_call" | custom-call | tf_op jit(solution)/shard_map/pack_kv/pallas_call | solution.py:109
  4.0 0.0 copy-start
  4.0 0.0 copy-start.1
  4.0 11.8 %all-to-all-start.1 = ((bf16[64,104,128]{2,1,0:T(8,128)(2,1)}), bf16[64,104,128]{2,1,0:T(8,128)(2,1)S(1)}, u32[]{:S(2)}, u32[]{:S(2)}) async-start(bf16[64,104,128]{2,1,0:T(8,128)(2,1)} %pack_kv.1), calls=%async_computation.1 | async-start | bytes 3407872 | tf_op jit(solution)/shard_map/all_to_all | solution.py:377
  15.8 0.0 copy-done
  15.8 0.0 copy-done.1
  15.8 4.4 %pack_q.1 = bf16[64,48,128]{2,1,0:T(8,128)(2,1)} custom-call(bf16[48,64]{1,0:T(8,128)(2,1)S(1)} %copy-done.1, bf16[48,64,128]{2,1,0:T(8,128)(2,1)S(1)} %copy-done), custom_call_target="tpu_custom_call" | custom-call | tf_op jit(solution)/shard_map/pack_q/pallas_call | solution.py:145
  20.2 37.2 %all-to-all-done.1.kv_ref = bf16[64,104,128]{2,1,0:T(8,128)(2,1)S(1)} async-done(((bf16[64,104,128]{2,1,0:T(8,128)(2,1)}), bf16[64,104,128]{2,1,0:T(8,128)(2,1)S(1)}, u32[]{:S(2)}, u32[]{:S(2)}) %all-to-all-start.1) | async-done | bytes 1703968 | tf_op jit(solution)/shard_map/all_to_all | solution.py:377
  57.4 6.7 %all-to-all-start = ((bf16[64,48,128]{2,1,0:T(8,128)(2,1)}), bf16[64,48,128]{2,1,0:T(8,128)(2,1)S(1)}, u32[]{:S(2)}, u32[]{:S(2)}) async-start(bf16[64,48,128]{2,1,0:T(8,128)(2,1)} %pack_q.1), calls=%async_computation | async-start | bytes 1572864 | tf_op jit(solution)/shard_map/all_to_all | solution.py:379
  64.1 0.7 states.1
  64.8 4.0 %collective-permute-start = (bf16[136,128]{1,0:T(8,128)(2,1)S(1)}, bf16[136,128]{1,0:T(8,128)(2,1)S(1)}, u32[]{:S(2)}, u32[]{:S(2)}) collective-permute-start(bf16[136,128]{1,0:T(8,128)(2,1)S(1)} %convert_element_type.19), channel_id=1, source_target_pairs={{0,64},{64,0},{128,192},{192,128},{256,320},{320,256},{384,448},{4... | collective-permute-start | bytes 104456 | tf_op jit(solution)/shard_map/ppermute | solution.py:358
  68.9 1.6 %collective-permute-done = bf16[136,128]{1,0:T(8,128)(2,1)S(1)} collective-permute-done((bf16[136,128]{1,0:T(8,128)(2,1)S(1)}, bf16[136,128]{1,0:T(8,128)(2,1)S(1)}, u32[]{:S(2)}, u32[]{:S(2)}) %collective-permute-start) | collective-permute-done | bytes 34848 | tf_op jit(solution)/shard_map/ppermute | solution.py:358
  70.5 5.8 %collective-permute-start.1 = (bf16[136,128]{1,0:T(8,128)(2,1)S(1)}, bf16[136,128]{1,0:T(8,128)(2,1)S(1)}, u32[]{:S(2)}, u32[]{:S(2)}) collective-permute-start(bf16[136,128]{1,0:T(8,128)(2,1)S(1)} %pad_maximum_fusion), channel_id=1, source_target_pairs={{0,128},{64,192},{128,0},{192,64},{256,384},{320,448},{384,256},{4... | collective-permute-start | bytes 104456 | tf_op jit(solution)/shard_map/ppermute | solution.py:358
  76.4 1.6 %collective-permute-done.1 = bf16[136,128]{1,0:T(8,128)(2,1)S(1)} collective-permute-done((bf16[136,128]{1,0:T(8,128)(2,1)S(1)}, bf16[136,128]{1,0:T(8,128)(2,1)S(1)}, u32[]{:S(2)}, u32[]{:S(2)}) %collective-permute-start.1) | collective-permute-done | bytes 34848 | tf_op jit(solution)/shard_map/ppermute | solution.py:358
  78.0 8.5 %collective-permute-start.2 = (bf16[136,128]{1,0:T(8,128)(2,1)S(1)}, bf16[136,128]{1,0:T(8,128)(2,1)S(1)}, u32[]{:S(2)}, u32[]{:S(2)}) collective-permute-start(bf16[136,128]{1,0:T(8,128)(2,1)S(1)} %pad_maximum_fusion.1), channel_id=1, source_target_pairs={{0,384},{64,448},{128,256},{192,320},{1,385},{65,449},{129,257},{1... | collective-permute-start | bytes 104456 | tf_op jit(solution)/shard_map/ppermute | solution.py:368
  86.5 1.0 collective-permute-done.2
  87.6 0.0 all-to-all-done.query_ref
  87.6 0.0 copy-start.2
  87.6 1.4 %attend.1 = bf16[64,48,128]{2,1,0:T(8,128)(2,1)S(1)} custom-call(bf16[64,48,128]{2,1,0:T(8,128)(2,1)S(1)} %all-to-all-done.query_ref, bf16[64,104,128]{2,1,0:T(8,128)(2,1)S(1)} %all-to-all-done.1.kv_ref, f32[8,128,128]{2,1,0:T(8,128)S(1)} %get-tuple-element.10.prefix_ref, f32[8,8,384]{2,1,0:T(8,128)S(1)} %get-tuple-element.11.factor_ref, ...), custom_call_target="tpu_custom_call" | custom-call | tf_op jit(solution)/shard_map/attend/pallas_call | solution.py:291
  89.0 35.5 %all_to_all.15.mixed_ref = bf16[64,48,128]{2,1,0:T(8,128)(2,1)S(1)} all-to-all(bf16[64,48,128]{2,1,0:T(8,128)(2,1)S(1)} %attend.1), channel_id=1, replica_groups=mesh['seg'=8,'sub'=8,'head'=8] {'head','sub'}, dimensions={0} | all-to-all | bytes 1572864 | tf_op jit(solution)/shard_map/all_to_all | solution.py:383
  124.5 0.0 copy-done.2
  124.5 2.0 %norm.1 = bf16[48,64,128]{2,1,0:T(8,128)(2,1)} custom-call(bf16[64,48,128]{2,1,0:T(8,128)(2,1)S(1)} %all_to_all.15.mixed_ref, f32[64,128]{1,0:T(8,128)S(1)} %copy-done.2), custom_call_target="tpu_custom_call" | custom-call | tf_op jit(solution)/shard_map/norm/pallas_call | solution.py:329
  (12 shorter events, 0.1 us)
Async XLA Ops:
  4.0 11.8 %copy-start = (bf16[48,64,128]{2,1,0:T(8,128)(2,1)S(1)}, bf16[48,64,128]{2,1,0:T(8,128)(2,1)}, u32[]{:S(2)}) copy-start(bf16[48,64,128]{2,1,0:T(8,128)(2,1)} %queries_ref.1) | copy-start | bytes 2359300
  4.0 11.8 %copy-start.1 = (bf16[48,64]{1,0:T(8,128)(2,1)S(1)}, bf16[48,64]{1,0:T(8,128)(2,1)}, u32[]{:S(2)}) copy-start(bf16[48,64]{1,0:T(8,128)(2,1)} %decay_hbm.1) | copy-start | bytes 18436
  4.0 53.4 %all-to-all-start.1 = ((bf16[64,104,128]{2,1,0:T(8,128)(2,1)}), bf16[64,104,128]{2,1,0:T(8,128)(2,1)S(1)}, u32[]{:S(2)}, u32[]{:S(2)}) async-start(bf16[64,104,128]{2,1,0:T(8,128)(2,1)} %pack_kv.1), calls=%async_computation.1 | async-start | bytes 3407872 | tf_op jit(solution)/shard_map/all_to_all | solution.py:377
  57.4 30.1 %all-to-all-start = ((bf16[64,48,128]{2,1,0:T(8,128)(2,1)}), bf16[64,48,128]{2,1,0:T(8,128)(2,1)S(1)}, u32[]{:S(2)}, u32[]{:S(2)}) async-start(bf16[64,48,128]{2,1,0:T(8,128)(2,1)} %pack_q.1), calls=%async_computation | async-start | bytes 1572864 | tf_op jit(solution)/shard_map/all_to_all | solution.py:379
  64.8 5.6 %collective-permute-start = (bf16[136,128]{1,0:T(8,128)(2,1)S(1)}, bf16[136,128]{1,0:T(8,128)(2,1)S(1)}, u32[]{:S(2)}, u32[]{:S(2)}) collective-permute-start(bf16[136,128]{1,0:T(8,128)(2,1)S(1)} %convert_element_type.19), channel_id=1, source_target_pairs={{0,64},{64,0},{128,192},{192,128},{256,320},{320,256},{384,448},{4... | collective-permute-start | bytes 104456 | tf_op jit(solution)/shard_map/ppermute | solution.py:358
  70.5 7.4 %collective-permute-start.1 = (bf16[136,128]{1,0:T(8,128)(2,1)S(1)}, bf16[136,128]{1,0:T(8,128)(2,1)S(1)}, u32[]{:S(2)}, u32[]{:S(2)}) collective-permute-start(bf16[136,128]{1,0:T(8,128)(2,1)S(1)} %pad_maximum_fusion), channel_id=1, source_target_pairs={{0,128},{64,192},{128,0},{192,64},{256,384},{320,448},{384,256},{4... | collective-permute-start | bytes 104456 | tf_op jit(solution)/shard_map/ppermute | solution.py:358
  78.0 9.5 %collective-permute-start.2 = (bf16[136,128]{1,0:T(8,128)(2,1)S(1)}, bf16[136,128]{1,0:T(8,128)(2,1)S(1)}, u32[]{:S(2)}, u32[]{:S(2)}) collective-permute-start(bf16[136,128]{1,0:T(8,128)(2,1)S(1)} %pad_maximum_fusion.1), channel_id=1, source_target_pairs={{0,384},{64,448},{128,256},{192,320},{1,385},{65,449},{129,257},{1... | collective-permute-start | bytes 104456 | tf_op jit(solution)/shard_map/ppermute | solution.py:368
  87.6 36.9 %copy-start.2 = (f32[64,128]{1,0:T(8,128)S(1)}, f32[64,128]{1,0:T(8,128)}, u32[]{:S(2)}) copy-start(f32[64,128]{1,0:T(8,128)} %gain_ref.1) | copy-start | bytes 98308

commit v4 on v3

--- a/solution.py
+++ b/solution.py
@@ -50,56 +50,58 @@
 
 def pack_kv_kernel(
     decay_hbm, keys_hbm, values_hbm, out_hbm,
-    decay, keys, values, key_rows, value_rows, to_end, totals, out, decay_sem, in_sem, out_sem,
+    decay, keys, values, key_rows, value_rows, out, decay_sem, in_sem, out_sem, extra_sem,
 ):
     tokens, heads, _ = keys.shape
     groups = heads // GROUP
 
-    def copies_in(g):
+    def copy_in(i, g):
+        source, target = ((values_hbm, values), (keys_hbm, keys))[i]
         columns = pl.ds(g * GROUP, GROUP)
-        return [
-            pltpu.make_async_copy(source.at[:, columns, :], target.at[:, columns, :], in_sem.at[i, g])
-            for i, (source, target) in enumerate(((keys_hbm, keys), (values_hbm, values)))
-        ]
-
-    def copy_out(g):
-        here = pl.ds(g * GROUP, GROUP)
-        return pltpu.make_async_copy(out.at[here], out_hbm.at[here], out_sem.at[g])
-
+        return pltpu.make_async_copy(source.at[:, columns, :], target.at[:, columns, :], in_sem.at[i, g])
+
+    def copy_out(i, g):
+        here, rows = pl.ds(g * GROUP, GROUP), pl.ds((1 - i) * tokens, tokens)
+        return pltpu.make_async_copy(out.at[here, rows, :], out_hbm.at[here, rows, :], out_sem.at[i, g])
+
+    extra = pl.ds(2 * tokens, EXTRA)
+    extra_out = pltpu.make_async_copy(out.at[:, extra, :], out_hbm.at[:, extra, :], extra_sem)
     decay_copy = pltpu.make_async_copy(decay_hbm, decay, decay_sem)
     decay_copy.start()
+    for i in range(2):
+        for g in range(groups):
+            copy_in(i, g).start()
     for g in range(groups):
-        for copy in copies_in(g):
-            copy.start()
+        copy_in(0, g).wait()
+        value_rows[...] = values[:, g * GROUP : (g + 1) * GROUP, :].astype(F32).reshape(tokens * GROUP, 128)
+        for j in range(GROUP):
+            value = value_rows[pl.ds(j, tokens, stride=GROUP), :]
+            out[g * GROUP + j, tokens : 2 * tokens, :] = silu(value).astype(BF16)
+        copy_out(0, g).start()
     decay_copy.wait()
     running = cumulative(decay[...])
-    to_end[...] = jnp.exp(running[tokens - 1 : tokens, :] - running)
+    to_end = jnp.exp(running[tokens - 1 : tokens, :] - running)
     row = iota((EXTRA, 128), 0)
     total = jnp.broadcast_to(running[tokens - 1 : tokens, :], (EXTRA, 128))
     high, middle, low = (part.astype(F32) for part in three_parts(total))
-    totals[...] = jnp.where(row == 0, high, jnp.where(row == 1, middle, jnp.where(row == 2, low, 0.0)))
-
-    def one(g, carry):
-        for copy in copies_in(g):
-            copy.wait()
-        columns = pl.ds(g * GROUP, GROUP)
-        scales, ends = group_lanes(to_end[...], g * GROUP), group_lanes(totals[...], g * GROUP)
-        key_rows[...] = keys[:, columns, :].astype(F32).reshape(tokens * GROUP, 128)
-        value_rows[...] = values[:, columns, :].astype(F32).reshape(tokens * GROUP, 128)
+    totals = jnp.where(row == 0, high, jnp.where(row == 1, middle, jnp.where(row == 2, low, 0.0)))
+    for head in range(heads):
+        end = jnp.broadcast_to(totals[:, head : head + 1], (EXTRA, 128))
+        out[head, 2 * tokens : 2 * tokens + EXTRA, :] = end.astype(BF16)
+    extra_out.start()
+    for g in range(groups):
+        copy_in(1, g).wait()
+        key_rows[...] = keys[:, g * GROUP : (g + 1) * GROUP, :].astype(F32).reshape(tokens * GROUP, 128)
         for j in range(GROUP):
-            rows = pl.ds(j, tokens, stride=GROUP)
             head = g * GROUP + j
-            scale = jnp.broadcast_to(scales[:, j : j + 1], (tokens, 128))
-            out[head, 0:tokens, :] = (silu(key_rows[rows, :]) * scale).astype(BF16)
-            out[head, tokens : 2 * tokens, :] = silu(value_rows[rows, :]).astype(BF16)
-            end = jnp.broadcast_to(ends[:, j : j + 1], (EXTRA, 128))
-            out[head, 2 * tokens : 2 * tokens + EXTRA, :] = end.astype(BF16)
-        copy_out(g).start()
-        return carry
-
-    lax.fori_loop(0, groups, one, 0)
-    for g in range(groups):
-        copy_out(g).wait()
+            scale = jnp.broadcast_to(to_end[:, head : head + 1], (tokens, 128))
+            key = key_rows[pl.ds(j, tokens, stride=GROUP), :]
+            out[head, 0:tokens, :] = (silu(key) * scale).astype(BF16)
+        copy_out(1, g).start()
+    for i in range(2):
+        for g in range(groups):
+            copy_out(i, g).wait()
+    extra_out.wait()
 
 
 def pack_kv(keys, values, decay):
@@ -117,12 +119,11 @@
             pltpu.VMEM(values.shape, BF16),
             pltpu.VMEM((tokens * GROUP, dim), F32),
             pltpu.VMEM((tokens * GROUP, dim), F32),
-            pltpu.VMEM((tokens, 128), F32),
-            pltpu.VMEM((EXTRA, 128), F32),
             pltpu.VMEM(packed, BF16),
             pltpu.SemaphoreType.DMA,
             pltpu.SemaphoreType.DMA((2, heads // GROUP)),
-            pltpu.SemaphoreType.DMA((heads // GROUP,)),
+            pltpu.SemaphoreType.DMA((2, heads // GROUP)),
+            pltpu.SemaphoreType.DMA,
         ],
         compiler_params=pltpu.CompilerParams(vmem_limit_bytes=FULL),
         name="pack_kv",
@@ -157,8 +158,18 @@
     )(decay, queries)
 
 
+def source_number(place, b, blocks):
+    return place * blocks + b % 2 * (blocks // 2) + b // 2
+
+
+def block_number(source, blocks):
+    within = source % blocks
+    return within % (blocks // 2) * 2 + within // (blocks // 2)
+
+
 def block_of(ref, b, blocks, first, last):
-    return jnp.concatenate([ref[i, first:last, :] for i in range(b, ref.shape[0], blocks)], axis=0)
+    places = ref.shape[0] // blocks
+    return jnp.concatenate([ref[source_number(p, b, blocks), first:last, :] for p in range(places)], axis=0)
 
 
 def states_kernel(per_block, kv_ref, prefix_ref, total_ref, factor_ref, enter_ref, reach_ref):
@@ -170,7 +181,7 @@
     totals = jnp.sum(tail, axis=1)
     parts = three_parts(totals)
     at, of = iota((sources, sources), 0), iota((sources, sources), 1)
-    same = at // per_block == of % blocks
+    same = at // per_block == block_number(of, blocks)
     at_place, of_place = at % per_block, of // blocks
 
     def mask(keep):
@@ -180,7 +191,7 @@
     after = dot_parts(mask(same & (of_place > at_place)), parts)
     enter_ref[...] = jnp.exp(before)
     to_block_end = jnp.exp(after)
-    block_at, source_of = iota((blocks, sources), 0), iota((blocks, sources), 1) % blocks
+    block_at, source_of = iota((blocks, sources), 0), block_number(iota((blocks, sources), 1), blocks)
     block_total = dot_parts(mask(block_at == source_of), parts)
     block_before = dot_parts(mask(block_at > source_of), parts)
     reach_ref[...] = jnp.exp(block_before)
@@ -202,7 +213,7 @@
         prefix_ref[b] = state
         keys = jnp.concatenate(
             [
-                kv_ref[p * blocks + b, 0:tokens, :].astype(F32) * to_block_end[b * per_block + p][None]
+                kv_ref[source_number(p, b, blocks), 0:tokens, :].astype(F32) * to_block_end[b * per_block + p][None]
                 for p in range(per_block)
             ],
             axis=0,
@@ -278,7 +289,7 @@
             for i in range(low // 16, high // 16):
                 source, row = divmod(i * 16, tokens)
                 piece = mixed[i * 16 - low : i * 16 - low + 16]
-                out_ref[source * blocks + b, row : row + 16, :] = piece
+                out_ref[source_number(source, b, blocks), row : row + 16, :] = piece
 
     tiles = weights(0)
     for b in range(blocks):
@@ -373,7 +384,7 @@
 
 def shards(queries, keys, values, decay_log, out_gain):
     per_block = lax.axis_size("head")
-    group = ("head", "sub")
+    group = ("head", "core", "chip")
     kv = lax.all_to_all(pack_kv(keys, values, decay_log), group, 0, 0, tiled=True)
     query = pack_q(queries, decay_log)
     query = lax.all_to_all(query, group, 0, 0, tiled=True)
@@ -389,8 +400,8 @@
     contexts, per_block = devices.shape
     heads = 64
     sub = heads // per_block
-    split = Mesh(devices.reshape(contexts // sub, sub, per_block), ("seg", "sub", "head"))
-    rows = ("seg", "sub", "head")
+    rows = ("seg", "chip", "core", "head")
+    split = Mesh(devices.reshape(contexts // sub, sub // 2, 2, per_block), rows)
     return jax.shard_map(
         shards,
         mesh=split,

time: 127 us -> 126 us (level)
  no operation moved by 1% of the time
where the time goes in v4:
time: 126 us
  waiting for transfers between devices  41.2 us (33%)
  starting transfers between devices  36.9 us (29%)
  blocking collectives  35.1 us (28%)
  Pallas kernels  12.1 us (10%)
    all_to_all x1, waiting for transfers between devices, shards(): lax.all_to_all(pack_kv(keys, values, decay_log), group, 0, 0, tiled=True)  36.9 us
    all_to_all x1, blocking collectives, shards(): mixed = lax.all_to_all(mixed, group, 0, 0, tiled=True)  35.1 us
    all_to_all x1, starting transfers between devices, shards(): lax.all_to_all(pack_kv(keys, values, decay_log), group, 0, 0, tiled=True)  11.8 us
    ppermute x2, starting transfers between devices, incoming_state(): lax.ppermute(mine, 'seg', [(i, i ^ hop) for i in range(count)])  9.81 us
    ppermute x1, starting transfers between devices, incoming_state(): lax.ppermute(whole.astype(BF16), 'seg', [(i, half + (i + half // 2) % hal...  8.47 us
    all_to_all x1, starting transfers between devices, shards(): query = lax.all_to_all(query, group, 0, 0, tiled=True)  6.9 us
    pallas_call x1, Pallas kernels, pack_q(): pl.pallas_call(pack_q_kernel, grid=(heads // 8,), in_specs=[pl.BlockSpec(...  4.4 us
    pallas_call x1, Pallas kernels, pack_kv(): pl.pallas_call(pack_kv_kernel, in_specs=[anywhere] * 3, out_specs=anywher...  3.55 us
  transfers between devices with their start and end apart: 5, of which 4 were waited for; matrix products, arithmetic and copies ran while one was open for 0% of the time, Pallas kernels for 4%

profile of v4, /device:TPU:1, one launch (start us, length us, event | category | flops | bytes accessed | tf_op | source)
XLA Modules:
  0.0 125.6 jit_solution(7162308494199567502)
XLA Ops:
  0.0 3.6 %pack_kv.1 = bf16[64,104,128]{2,1,0:T(8,128)(2,1)} custom-call(bf16[48,64]{1,0:T(8,128)(2,1)} %decay_hbm.1, bf16[48,64,128]{2,1,0:T(8,128)(2,1)} %keys_hbm.1, bf16[48,64,128]{2,1,0:T(8,128)(2,1)} %values_hbm.1), custom_call_target="tpu_custom_call" | custom-call | tf_op jit(solution)/shard_map/pack_kv/pallas_call | solution.py:111
  3.6 0.0 copy-start
  3.6 0.0 copy-start.1
  3.6 11.8 %all-to-all-start.1 = ((bf16[64,104,128]{2,1,0:T(8,128)(2,1)}), bf16[64,104,128]{2,1,0:T(8,128)(2,1)S(1)}, u32[]{:S(2)}, u32[]{:S(2)}) async-start(bf16[64,104,128]{2,1,0:T(8,128)(2,1)} %pack_kv.1), calls=%async_computation.1 | async-start | bytes 3407872 | tf_op jit(solution)/shard_map/all_to_all | solution.py:388
  15.4 0.0 copy-done
  15.4 0.0 copy-done.1
  15.4 4.4 %pack_q.1 = bf16[64,48,128]{2,1,0:T(8,128)(2,1)} custom-call(bf16[48,64]{1,0:T(8,128)(2,1)S(1)} %copy-done.1, bf16[48,64,128]{2,1,0:T(8,128)(2,1)S(1)} %copy-done), custom_call_target="tpu_custom_call" | custom-call | tf_op jit(solution)/shard_map/pack_q/pallas_call | solution.py:146
  19.8 36.9 %all-to-all-done.1.kv_ref = bf16[64,104,128]{2,1,0:T(8,128)(2,1)S(1)} async-done(((bf16[64,104,128]{2,1,0:T(8,128)(2,1)}), bf16[64,104,128]{2,1,0:T(8,128)(2,1)S(1)}, u32[]{:S(2)}, u32[]{:S(2)}) %all-to-all-start.1) | async-done | bytes 1703968 | tf_op jit(solution)/shard_map/all_to_all | solution.py:388
  56.7 6.9 %all-to-all-start = ((bf16[64,48,128]{2,1,0:T(8,128)(2,1)}), bf16[64,48,128]{2,1,0:T(8,128)(2,1)S(1)}, u32[]{:S(2)}, u32[]{:S(2)}) async-start(bf16[64,48,128]{2,1,0:T(8,128)(2,1)} %pack_q.1), calls=%async_computation | async-start | bytes 1572864 | tf_op jit(solution)/shard_map/all_to_all | solution.py:390
  63.6 0.7 states.1
  64.4 4.0 %collective-permute-start = (bf16[136,128]{1,0:T(8,128)(2,1)S(1)}, bf16[136,128]{1,0:T(8,128)(2,1)S(1)}, u32[]{:S(2)}, u32[]{:S(2)}) collective-permute-start(bf16[136,128]{1,0:T(8,128)(2,1)S(1)} %convert_element_type.19), channel_id=1, source_target_pairs={{0,64},{64,0},{128,192},{192,128},{256,320},{320,256},{384,448},{4... | collective-permute-start | bytes 104456 | tf_op jit(solution)/shard_map/ppermute | solution.py:369
  68.4 1.6 %collective-permute-done = bf16[136,128]{1,0:T(8,128)(2,1)S(1)} collective-permute-done((bf16[136,128]{1,0:T(8,128)(2,1)S(1)}, bf16[136,128]{1,0:T(8,128)(2,1)S(1)}, u32[]{:S(2)}, u32[]{:S(2)}) %collective-permute-start) | collective-permute-done | bytes 34848 | tf_op jit(solution)/shard_map/ppermute | solution.py:369
  70.1 5.8 %collective-permute-start.1 = (bf16[136,128]{1,0:T(8,128)(2,1)S(1)}, bf16[136,128]{1,0:T(8,128)(2,1)S(1)}, u32[]{:S(2)}, u32[]{:S(2)}) collective-permute-start(bf16[136,128]{1,0:T(8,128)(2,1)S(1)} %pad_maximum_fusion), channel_id=1, source_target_pairs={{0,128},{64,192},{128,0},{192,64},{256,384},{320,448},{384,256},{4... | collective-permute-start | bytes 104456 | tf_op jit(solution)/shard_map/ppermute | solution.py:369
  75.9 1.6 %collective-permute-done.1 = bf16[136,128]{1,0:T(8,128)(2,1)S(1)} collective-permute-done((bf16[136,128]{1,0:T(8,128)(2,1)S(1)}, bf16[136,128]{1,0:T(8,128)(2,1)S(1)}, u32[]{:S(2)}, u32[]{:S(2)}) %collective-permute-start.1) | collective-permute-done | bytes 34848 | tf_op jit(solution)/shard_map/ppermute | solution.py:369
  77.6 8.5 %collective-permute-start.2 = (bf16[136,128]{1,0:T(8,128)(2,1)S(1)}, bf16[136,128]{1,0:T(8,128)(2,1)S(1)}, u32[]{:S(2)}, u32[]{:S(2)}) collective-permute-start(bf16[136,128]{1,0:T(8,128)(2,1)S(1)} %pad_maximum_fusion.1), channel_id=1, source_target_pairs={{0,384},{64,448},{128,256},{192,320},{1,385},{65,449},{129,257},{1... | collective-permute-start | bytes 104456 | tf_op jit(solution)/shard_map/ppermute | solution.py:379
  86.0 1.0 collective-permute-done.2
  87.1 0.0 all-to-all-done.query_ref
  87.1 0.0 copy-start.2
  87.1 1.4 %attend.1 = bf16[64,48,128]{2,1,0:T(8,128)(2,1)S(1)} custom-call(bf16[64,48,128]{2,1,0:T(8,128)(2,1)S(1)} %all-to-all-done.query_ref, bf16[64,104,128]{2,1,0:T(8,128)(2,1)S(1)} %all-to-all-done.1.kv_ref, f32[8,128,128]{2,1,0:T(8,128)S(1)} %get-tuple-element.10.prefix_ref, f32[8,8,384]{2,1,0:T(8,128)S(1)} %get-tuple-element.11.factor_ref, ...), custom_call_target="tpu_custom_call" | custom-call | tf_op jit(solution)/shard_map/attend/pallas_call | solution.py:302
  88.5 35.1 %all_to_all.15.mixed_ref = bf16[64,48,128]{2,1,0:T(8,128)(2,1)S(1)} all-to-all(bf16[64,48,128]{2,1,0:T(8,128)(2,1)S(1)} %attend.1), channel_id=1, replica_groups=mesh['seg'=8,'chip'=4,'core'=2,'head'=8] {'head','core','chip'}, dimensions={0} | all-to-all | bytes 1572864 | tf_op jit(solution)/shard_map/all_to_all | solution.py:394
  123.6 0.0 copy-done.2
  123.6 2.0 %norm.1 = bf16[48,64,128]{2,1,0:T(8,128)(2,1)} custom-call(bf16[64,48,128]{2,1,0:T(8,128)(2,1)S(1)} %all_to_all.15.mixed_ref, f32[64,128]{1,0:T(8,128)S(1)} %copy-done.2), custom_call_target="tpu_custom_call" | custom-call | tf_op jit(solution)/shard_map/norm/pallas_call | solution.py:340
  (12 shorter events, 0.1 us)
Async XLA Ops:
  3.6 11.8 %copy-start = (bf16[48,64,128]{2,1,0:T(8,128)(2,1)S(1)}, bf16[48,64,128]{2,1,0:T(8,128)(2,1)}, u32[]{:S(2)}) copy-start(bf16[48,64,128]{2,1,0:T(8,128)(2,1)} %queries_ref.1) | copy-start | bytes 2359300
  3.6 11.8 %copy-start.1 = (bf16[48,64]{1,0:T(8,128)(2,1)S(1)}, bf16[48,64]{1,0:T(8,128)(2,1)}, u32[]{:S(2)}) copy-start(bf16[48,64]{1,0:T(8,128)(2,1)} %decay_hbm.1) | copy-start | bytes 18436
  3.6 53.1 %all-to-all-start.1 = ((bf16[64,104,128]{2,1,0:T(8,128)(2,1)}), bf16[64,104,128]{2,1,0:T(8,128)(2,1)S(1)}, u32[]{:S(2)}, u32[]{:S(2)}) async-start(bf16[64,104,128]{2,1,0:T(8,128)(2,1)} %pack_kv.1), calls=%async_computation.1 | async-start | bytes 3407872 | tf_op jit(solution)/shard_map/all_to_all | solution.py:388
  56.7 30.4 %all-to-all-start = ((bf16[64,48,128]{2,1,0:T(8,128)(2,1)}), bf16[64,48,128]{2,1,0:T(8,128)(2,1)S(1)}, u32[]{:S(2)}, u32[]{:S(2)}) async-start(bf16[64,48,128]{2,1,0:T(8,128)(2,1)} %pack_q.1), calls=%async_computation | async-start | bytes 1572864 | tf_op jit(solution)/shard_map/all_to_all | solution.py:390
  64.4 5.6 %collective-permute-start = (bf16[136,128]{1,0:T(8,128)(2,1)S(1)}, bf16[136,128]{1,0:T(8,128)(2,1)S(1)}, u32[]{:S(2)}, u32[]{:S(2)}) collective-permute-start(bf16[136,128]{1,0:T(8,128)(2,1)S(1)} %convert_element_type.19), channel_id=1, source_target_pairs={{0,64},{64,0},{128,192},{192,128},{256,320},{320,256},{384,448},{4... | collective-permute-start | bytes 104456 | tf_op jit(solution)/shard_map/ppermute | solution.py:369
  70.1 7.4 %collective-permute-start.1 = (bf16[136,128]{1,0:T(8,128)(2,1)S(1)}, bf16[136,128]{1,0:T(8,128)(2,1)S(1)}, u32[]{:S(2)}, u32[]{:S(2)}) collective-permute-start(bf16[136,128]{1,0:T(8,128)(2,1)S(1)} %pad_maximum_fusion), channel_id=1, source_target_pairs={{0,128},{64,192},{128,0},{192,64},{256,384},{320,448},{384,256},{4... | collective-permute-start | bytes 104456 | tf_op jit(solution)/shard_map/ppermute | solution.py:369
  77.6 9.5 %collective-permute-start.2 = (bf16[136,128]{1,0:T(8,128)(2,1)S(1)}, bf16[136,128]{1,0:T(8,128)(2,1)S(1)}, u32[]{:S(2)}, u32[]{:S(2)}) collective-permute-start(bf16[136,128]{1,0:T(8,128)(2,1)S(1)} %pad_maximum_fusion.1), channel_id=1, source_target_pairs={{0,384},{64,448},{128,256},{192,320},{1,385},{65,449},{129,257},{1... | collective-permute-start | bytes 104456 | tf_op jit(solution)/shard_map/ppermute | solution.py:379
  87.1 36.5 %copy-start.2 = (f32[64,128]{1,0:T(8,128)S(1)}, f32[64,128]{1,0:T(8,128)}, u32[]{:S(2)}) copy-start(f32[64,128]{1,0:T(8,128)} %gain_ref.1) | copy-start | bytes 98308

commit v5 on v4

--- a/solution.py
+++ b/solution.py
@@ -361,12 +361,13 @@
     dim = own.shape[1]
     segment = lax.axis_index("seg")
     count = lax.axis_size("seg")
+    half, quarter = count // 2, count // 4
+    pairs = [(i, i ^ 1) for i in range(count)]
+    upward = [(i, i + quarter) for i in range(count) if i % half < quarter]
     whole = own
     entering_state, entering_decay = jnp.zeros((dim, dim), F32), jnp.ones((1, dim), F32)
-    hop = 1
-    while hop < count // 2:
-        mine = whole.astype(BF16)
-        state, decay = received(lax.ppermute(mine, "seg", [(i, i ^ hop) for i in range(count)]))
+    for hop, moves in ((1, pairs), (quarter, upward)):
+        state, decay = received(lax.ppermute(whole.astype(BF16), "seg", moves))
         upper = ((segment & hop) != 0).astype(F32)
         lower = 1.0 - upper
         entering_state = (upper * entering_decay) * state + entering_state
@@ -374,12 +375,9 @@
         own_decay = whole[dim : dim + 1]
         joined = (upper * own_decay + lower) * state + (lower * decay + upper) * whole[:dim]
         whole = jnp.concatenate([joined, jnp.broadcast_to(decay * own_decay, (EXTRA, dim))], axis=0)
-        hop *= 2
-    half = count // 2
-    state, _ = received(lax.ppermute(
-        whole.astype(BF16), "seg", [(i, half + (i + half // 2) % half) for i in range(half)]
-    ))
-    return entering_decay * state + entering_state
+    near = lax.ppermute(whole[:dim].astype(BF16), "seg", [(i, i + quarter) for i in range(quarter, half)])
+    far = lax.ppermute(near, "seg", [(i, i + quarter) for i in range(half, half + quarter)])
+    return entering_decay * (near.astype(F32) + far.astype(F32)) + entering_state
 
 
 def shards(queries, keys, values, decay_log, out_gain):

time: 126 us -> 125 us (level)
  the two profiles are of different devices: /device:TPU:1 before, /device:TPU:448 now
where the time goes in v5:
time: 125 us; the launch traced here: 124 us
  waiting for transfers between devices  56.5 us (45%)
  blocking collectives  33.5 us (27%)
  starting transfers between devices  21.7 us (17%)
  Pallas kernels  12.1 us (10%)
    all_to_all x1, waiting for transfers between devices, shards(): lax.all_to_all(pack_kv(keys, values, decay_log), group, 0, 0, tiled=True)  38.5 us
    all_to_all x1, blocking collectives, shards(): mixed = lax.all_to_all(mixed, group, 0, 0, tiled=True)  33.5 us
    all_to_all x1, starting transfers between devices, shards(): lax.all_to_all(pack_kv(keys, values, decay_log), group, 0, 0, tiled=True)  10.7 us
    ppermute x2, waiting for transfers between devices, incoming_state(): state, decay = received(lax.ppermute(whole.astype(BF16), 'seg', moves))  9.14 us
    ppermute x1, waiting for transfers between devices, incoming_state(): lax.ppermute(near, 'seg', [(i, i + quarter) for i in range(half, half + q...  8.79 us
    all_to_all x1, starting transfers between devices, shards(): query = lax.all_to_all(query, group, 0, 0, tiled=True)  5.32 us
    pallas_call x1, Pallas kernels, pack_q(): pl.pallas_call(pack_q_kernel, grid=(heads // 8,), in_specs=[pl.BlockSpec(...  4.4 us
    ppermute x2, starting transfers between devices, incoming_state(): state, decay = received(lax.ppermute(whole.astype(BF16), 'seg', moves))  3.75 us
  transfers between devices with their start and end apart: 6, of which 4 were waited for; matrix products, arithmetic and copies ran while one was open for 0% of the time, Pallas kernels for 4%

profile of v5, /device:TPU:448, one launch (start us, length us, event | category | flops | bytes accessed | tf_op | source)
XLA Modules:
  0.0 124.1 jit_solution(14118168137068060798)
XLA Ops:
  0.0 3.5 %pack_kv.1 = bf16[64,104,128]{2,1,0:T(8,128)(2,1)} custom-call(bf16[48,64]{1,0:T(8,128)(2,1)} %decay_hbm.1, bf16[48,64,128]{2,1,0:T(8,128)(2,1)} %keys_hbm.1, bf16[48,64,128]{2,1,0:T(8,128)(2,1)} %values_hbm.1), custom_call_target="tpu_custom_call" | custom-call | tf_op jit(solution)/shard_map/pack_kv/pallas_call | solution.py:111
  3.6 0.0 copy-start
  3.6 0.0 copy-start.1
  3.6 10.7 %all-to-all-start.1 = ((bf16[64,104,128]{2,1,0:T(8,128)(2,1)}), bf16[64,104,128]{2,1,0:T(8,128)(2,1)S(1)}, u32[]{:S(2)}, u32[]{:S(2)}) async-start(bf16[64,104,128]{2,1,0:T(8,128)(2,1)} %pack_kv.1), calls=%async_computation.1 | async-start | bytes 3407872 | tf_op jit(solution)/shard_map/all_to_all | solution.py:386
  14.3 0.0 copy-done
  14.3 0.0 copy-done.1
  14.3 4.4 %pack_q.1 = bf16[64,48,128]{2,1,0:T(8,128)(2,1)} custom-call(bf16[48,64]{1,0:T(8,128)(2,1)S(1)} %copy-done.1, bf16[48,64,128]{2,1,0:T(8,128)(2,1)S(1)} %copy-done), custom_call_target="tpu_custom_call" | custom-call | tf_op jit(solution)/shard_map/pack_q/pallas_call | solution.py:146
  18.7 38.5 %all-to-all-done.1.kv_ref = bf16[64,104,128]{2,1,0:T(8,128)(2,1)S(1)} async-done(((bf16[64,104,128]{2,1,0:T(8,128)(2,1)}), bf16[64,104,128]{2,1,0:T(8,128)(2,1)S(1)}, u32[]{:S(2)}, u32[]{:S(2)}) %all-to-all-start.1) | async-done | bytes 1703968 | tf_op jit(solution)/shard_map/all_to_all | solution.py:386
  57.2 5.3 %all-to-all-start = ((bf16[64,48,128]{2,1,0:T(8,128)(2,1)}), bf16[64,48,128]{2,1,0:T(8,128)(2,1)S(1)}, u32[]{:S(2)}, u32[]{:S(2)}) async-start(bf16[64,48,128]{2,1,0:T(8,128)(2,1)} %pack_q.1), calls=%async_computation | async-start | bytes 1572864 | tf_op jit(solution)/shard_map/all_to_all | solution.py:388
  62.6 0.7 states.1
  63.3 2.5 %collective-permute-start = (bf16[136,128]{1,0:T(8,128)(2,1)S(1)}, bf16[136,128]{1,0:T(8,128)(2,1)S(1)}, u32[]{:S(2)}, u32[]{:S(2)}) collective-permute-start(bf16[136,128]{1,0:T(8,128)(2,1)S(1)} %convert_element_type.26), channel_id=1, source_target_pairs={{0,64},{64,0},{128,192},{192,128},{256,320},{320,256},{384,448},{4... | collective-permute-start | bytes 104456 | tf_op jit(solution)/shard_map/ppermute | solution.py:370
  65.8 3.4 %collective-permute-done = bf16[136,128]{1,0:T(8,128)(2,1)S(1)} collective-permute-done((bf16[136,128]{1,0:T(8,128)(2,1)S(1)}, bf16[136,128]{1,0:T(8,128)(2,1)S(1)}, u32[]{:S(2)}, u32[]{:S(2)}) %collective-permute-start) | collective-permute-done | bytes 34848 | tf_op jit(solution)/shard_map/ppermute | solution.py:370
  69.2 1.3 %collective-permute-start.1 = (bf16[136,128]{1,0:T(8,128)(2,1)S(1)}, bf16[136,128]{1,0:T(8,128)(2,1)S(1)}, u32[]{:S(2)}, u32[]{:S(2)}) collective-permute-start(bf16[136,128]{1,0:T(8,128)(2,1)S(1)} %pad_maximum_fusion), channel_id=1, source_target_pairs={{0,128},{64,192},{256,384},{320,448},{1,129},{65,193},{257,385},{3... | collective-permute-start | bytes 104456 | tf_op jit(solution)/shard_map/ppermute | solution.py:370
  70.5 5.8 %collective-permute-done.1 = bf16[136,128]{1,0:T(8,128)(2,1)S(1)} collective-permute-done((bf16[136,128]{1,0:T(8,128)(2,1)S(1)}, bf16[136,128]{1,0:T(8,128)(2,1)S(1)}, u32[]{:S(2)}, u32[]{:S(2)}) %collective-permute-start.1) | collective-permute-done | bytes 34848 | tf_op jit(solution)/shard_map/ppermute | solution.py:370
  76.4 0.7 collective-permute-start.2
  77.0 0.0 collective-permute-done.2
  77.1 1.3 %collective-permute-start.3 = (bf16[128,128]{1,0:T(8,128)(2,1)S(1)}, bf16[128,128]{1,0:T(8,128)(2,1)S(1)}, u32[]{:S(2)}, u32[]{:S(2)}) collective-permute-start(bf16[128,128]{1,0:T(8,128)(2,1)S(1)} %collective-permute-done.2), channel_id=1, source_target_pairs={{256,384},{320,448},{257,385},{321,449},{258,386},{322,450},{259,3... | collective-permute-start | bytes 98312 | tf_op jit(solution)/shard_map/ppermute | solution.py:379
  78.4 8.8 %collective-permute-done.3 = bf16[128,128]{1,0:T(8,128)(2,1)S(1)} collective-permute-done((bf16[128,128]{1,0:T(8,128)(2,1)S(1)}, bf16[128,128]{1,0:T(8,128)(2,1)S(1)}, u32[]{:S(2)}, u32[]{:S(2)}) %collective-permute-start.3) | collective-permute-done | bytes 32800 | tf_op jit(solution)/shard_map/ppermute | solution.py:379
  87.2 0.0 all-to-all-done.query_ref
  87.2 0.0 copy-start.2
  87.2 1.4 %attend.1 = bf16[64,48,128]{2,1,0:T(8,128)(2,1)S(1)} custom-call(bf16[64,48,128]{2,1,0:T(8,128)(2,1)S(1)} %all-to-all-done.query_ref, bf16[64,104,128]{2,1,0:T(8,128)(2,1)S(1)} %all-to-all-done.1.kv_ref, f32[8,128,128]{2,1,0:T(8,128)S(1)} %get-tuple-element.10.prefix_ref, f32[8,8,384]{2,1,0:T(8,128)S(1)} %get-tuple-element.11.factor_ref, ...), custom_call_target="tpu_custom_call" | custom-call | tf_op jit(solution)/shard_map/attend/pallas_call | solution.py:302
  88.6 33.5 %all_to_all.15.mixed_ref = bf16[64,48,128]{2,1,0:T(8,128)(2,1)S(1)} all-to-all(bf16[64,48,128]{2,1,0:T(8,128)(2,1)S(1)} %attend.1), channel_id=1, replica_groups=mesh['seg'=8,'chip'=4,'core'=2,'head'=8] {'head','core','chip'}, dimensions={0} | all-to-all | bytes 1572864 | tf_op jit(solution)/shard_map/all_to_all | solution.py:392
  122.1 0.0 copy-done.2
  122.1 2.0 %norm.1 = bf16[48,64,128]{2,1,0:T(8,128)(2,1)} custom-call(bf16[64,48,128]{2,1,0:T(8,128)(2,1)S(1)} %all_to_all.15.mixed_ref, f32[64,128]{1,0:T(8,128)S(1)} %copy-done.2), custom_call_target="tpu_custom_call" | custom-call | tf_op jit(solution)/shard_map/norm/pallas_call | solution.py:340
  (10 shorter events, 0.1 us)
Async XLA Ops:
  3.6 10.7 %copy-start = (bf16[48,64,128]{2,1,0:T(8,128)(2,1)S(1)}, bf16[48,64,128]{2,1,0:T(8,128)(2,1)}, u32[]{:S(2)}) copy-start(bf16[48,64,128]{2,1,0:T(8,128)(2,1)} %queries_ref.1) | copy-start | bytes 2359300
  3.6 10.7 %copy-start.1 = (bf16[48,64]{1,0:T(8,128)(2,1)S(1)}, bf16[48,64]{1,0:T(8,128)(2,1)}, u32[]{:S(2)}) copy-start(bf16[48,64]{1,0:T(8,128)(2,1)} %decay_hbm.1) | copy-start | bytes 18436
  3.6 53.7 %all-to-all-start.1 = ((bf16[64,104,128]{2,1,0:T(8,128)(2,1)}), bf16[64,104,128]{2,1,0:T(8,128)(2,1)S(1)}, u32[]{:S(2)}, u32[]{:S(2)}) async-start(bf16[64,104,128]{2,1,0:T(8,128)(2,1)} %pack_kv.1), calls=%async_computation.1 | async-start | bytes 3407872 | tf_op jit(solution)/shard_map/all_to_all | solution.py:386
  57.2 29.9 %all-to-all-start = ((bf16[64,48,128]{2,1,0:T(8,128)(2,1)}), bf16[64,48,128]{2,1,0:T(8,128)(2,1)S(1)}, u32[]{:S(2)}, u32[]{:S(2)}) async-start(bf16[64,48,128]{2,1,0:T(8,128)(2,1)} %pack_q.1), calls=%async_computation | async-start | bytes 1572864 | tf_op jit(solution)/shard_map/all_to_all | solution.py:388
  63.3 5.8 %collective-permute-start = (bf16[136,128]{1,0:T(8,128)(2,1)S(1)}, bf16[136,128]{1,0:T(8,128)(2,1)S(1)}, u32[]{:S(2)}, u32[]{:S(2)}) collective-permute-start(bf16[136,128]{1,0:T(8,128)(2,1)S(1)} %convert_element_type.26), channel_id=1, source_target_pairs={{0,64},{64,0},{128,192},{192,128},{256,320},{320,256},{384,448},{4... | collective-permute-start | bytes 104456 | tf_op jit(solution)/shard_map/ppermute | solution.py:370
  69.2 7.1 %collective-permute-start.1 = (bf16[136,128]{1,0:T(8,128)(2,1)S(1)}, bf16[136,128]{1,0:T(8,128)(2,1)S(1)}, u32[]{:S(2)}, u32[]{:S(2)}) collective-permute-start(bf16[136,128]{1,0:T(8,128)(2,1)S(1)} %pad_maximum_fusion), channel_id=1, source_target_pairs={{0,128},{64,192},{256,384},{320,448},{1,129},{65,193},{257,385},{3... | collective-permute-start | bytes 104456 | tf_op jit(solution)/shard_map/ppermute | solution.py:370
  76.4 0.7 collective-permute-start.2
  77.1 10.1 %collective-permute-start.3 = (bf16[128,128]{1,0:T(8,128)(2,1)S(1)}, bf16[128,128]{1,0:T(8,128)(2,1)S(1)}, u32[]{:S(2)}, u32[]{:S(2)}) collective-permute-start(bf16[128,128]{1,0:T(8,128)(2,1)S(1)} %collective-permute-done.2), channel_id=1, source_target_pairs={{256,384},{320,448},{257,385},{321,449},{258,386},{322,450},{259,3... | collective-permute-start | bytes 98312 | tf_op jit(solution)/shard_map/ppermute | solution.py:379
  87.2 35.0 %copy-start.2 = (f32[64,128]{1,0:T(8,128)S(1)}, f32[64,128]{1,0:T(8,128)}, u32[]{:S(2)}) copy-start(f32[64,128]{1,0:T(8,128)} %gain_ref.1) | copy-start | bytes 98308

commit v6 on v5

--- a/solution.py
+++ b/solution.py
@@ -360,24 +360,26 @@
 def incoming_state(own):
     dim = own.shape[1]
     segment = lax.axis_index("seg")
-    count = lax.axis_size("seg")
-    half, quarter = count // 2, count // 4
-    pairs = [(i, i ^ 1) for i in range(count)]
-    upward = [(i, i + quarter) for i in range(count) if i % half < quarter]
-    whole = own
-    entering_state, entering_decay = jnp.zeros((dim, dim), F32), jnp.ones((1, dim), F32)
-    for hop, moves in ((1, pairs), (quarter, upward)):
-        state, decay = received(lax.ppermute(whole.astype(BF16), "seg", moves))
-        upper = ((segment & hop) != 0).astype(F32)
-        lower = 1.0 - upper
-        entering_state = (upper * entering_decay) * state + entering_state
-        entering_decay = entering_decay * (upper * decay + lower)
-        own_decay = whole[dim : dim + 1]
-        joined = (upper * own_decay + lower) * state + (lower * decay + upper) * whole[:dim]
-        whole = jnp.concatenate([joined, jnp.broadcast_to(decay * own_decay, (EXTRA, dim))], axis=0)
-    near = lax.ppermute(whole[:dim].astype(BF16), "seg", [(i, i + quarter) for i in range(quarter, half)])
-    far = lax.ppermute(near, "seg", [(i, i + quarter) for i in range(half, half + quarter)])
-    return entering_decay * (near.astype(F32) + far.astype(F32)) + entering_state
+    odd = (segment & 1).astype(F32)
+    second = ((segment & 2) != 0).astype(F32)
+    rows = dim + EXTRA
+    state, decay = received(lax.ppermute(own.astype(BF16), "seg", [(i, i ^ 1) for i in range(8)]))
+    entering_state, entering_decay = odd * state, odd * decay + (1.0 - odd)
+    own_decay = own[dim : dim + 1]
+    joined = (odd * own_decay + (1.0 - odd)) * state + ((1.0 - odd) * decay + odd) * own[:dim]
+    pair = jnp.concatenate([joined, jnp.broadcast_to(decay * own_decay, (EXTRA, dim))], axis=0).astype(BF16)
+    first = lax.ppermute(pair, "seg", [(0, 6), (1, 7), (2, 4), (3, 5)])
+    both = lax.ppermute(
+        jnp.concatenate([pair, first], axis=0), "seg", [(0, 2), (1, 3), (4, 6), (5, 7), (6, 4), (7, 5)]
+    )
+    mine, mine_decay = received(first)
+    before, before_decay = received(both[:rows])
+    theirs, theirs_decay = received(both[rows:])
+    early = second * mine + (1.0 - second) * theirs
+    late, late_decay = second * theirs + (1.0 - second) * mine, second * theirs_decay + (1.0 - second) * mine_decay
+    state = late + late_decay * early
+    state = second * before + (second * before_decay + (1.0 - second)) * state
+    return entering_decay * state + entering_state
 
 
 def shards(queries, keys, values, decay_log, out_gain):

time: 125 us -> 124 us (level)
  the two profiles are of different devices: /device:TPU:448 before, /device:TPU:1 now
where the time goes in v6:
time: 124 us; the launch traced here: 123 us
  waiting for transfers between devices  42.2 us (34%)
  starting transfers between devices  34.8 us (28%)
  blocking collectives  33.7 us (27%)
  Pallas kernels  12.1 us (10%)
    all_to_all x1, waiting for transfers between devices, shards(): lax.all_to_all(pack_kv(keys, values, decay_log), group, 0, 0, tiled=True)  36.9 us
    all_to_all x1, blocking collectives, shards(): mixed = lax.all_to_all(mixed, group, 0, 0, tiled=True)  33.7 us
    all_to_all x1, starting transfers between devices, shards(): lax.all_to_all(pack_kv(keys, values, decay_log), group, 0, 0, tiled=True)  11.8 us
    ppermute x1, starting transfers between devices, incoming_state(): first = lax.ppermute(pair, 'seg', [(0, 6), (1, 7), (2, 4), (3, 5)])  10 us
    all_to_all x1, starting transfers between devices, shards(): query = lax.all_to_all(query, group, 0, 0, tiled=True)  6.9 us
    pallas_call x1, Pallas kernels, pack_q(): pl.pallas_call(pack_q_kernel, grid=(heads // 8,), in_specs=[pl.BlockSpec(...  4.4 us
    ppermute x1, starting transfers between devices, incoming_state(): lax.ppermute(own.astype(BF16), 'seg', [(i, i ^ 1) for i in range(8)])  3.99 us
    pallas_call x1, Pallas kernels, pack_kv(): pl.pallas_call(pack_kv_kernel, in_specs=[anywhere] * 3, out_specs=anywher...  3.55 us
  transfers between devices with their start and end apart: 5, of which 5 were waited for; matrix products, arithmetic and copies ran while one was open for 0% of the time, Pallas kernels for 4%

profile of v6, /device:TPU:1, one launch (start us, length us, event | category | flops | bytes accessed | tf_op | source)
XLA Modules:
  0.0 123.1 jit_solution(1165636172057810370)
XLA Ops:
  0.0 3.5 %pack_kv.1 = bf16[64,104,128]{2,1,0:T(8,128)(2,1)} custom-call(bf16[48,64]{1,0:T(8,128)(2,1)} %decay_hbm.1, bf16[48,64,128]{2,1,0:T(8,128)(2,1)} %keys_hbm.1, bf16[48,64,128]{2,1,0:T(8,128)(2,1)} %values_hbm.1), custom_call_target="tpu_custom_call" | custom-call | tf_op jit(solution)/shard_map/pack_kv/pallas_call | solution.py:111
  3.6 0.0 copy-start
  3.6 0.0 copy-start.1
  3.6 11.8 %all-to-all-start.1 = ((bf16[64,104,128]{2,1,0:T(8,128)(2,1)}), bf16[64,104,128]{2,1,0:T(8,128)(2,1)S(1)}, u32[]{:S(2)}, u32[]{:S(2)}) async-start(bf16[64,104,128]{2,1,0:T(8,128)(2,1)} %pack_kv.1), calls=%async_computation.1 | async-start | bytes 3407872 | tf_op jit(solution)/shard_map/all_to_all | solution.py:388
  15.4 0.0 copy-done
  15.4 0.0 copy-done.1
  15.4 4.4 %pack_q.1 = bf16[64,48,128]{2,1,0:T(8,128)(2,1)} custom-call(bf16[48,64]{1,0:T(8,128)(2,1)S(1)} %copy-done.1, bf16[48,64,128]{2,1,0:T(8,128)(2,1)S(1)} %copy-done), custom_call_target="tpu_custom_call" | custom-call | tf_op jit(solution)/shard_map/pack_q/pallas_call | solution.py:146
  19.8 36.9 %all-to-all-done.1.kv_ref = bf16[64,104,128]{2,1,0:T(8,128)(2,1)S(1)} async-done(((bf16[64,104,128]{2,1,0:T(8,128)(2,1)}), bf16[64,104,128]{2,1,0:T(8,128)(2,1)S(1)}, u32[]{:S(2)}, u32[]{:S(2)}) %all-to-all-start.1) | async-done | bytes 1703968 | tf_op jit(solution)/shard_map/all_to_all | solution.py:388
  56.7 6.9 %all-to-all-start = ((bf16[64,48,128]{2,1,0:T(8,128)(2,1)}), bf16[64,48,128]{2,1,0:T(8,128)(2,1)S(1)}, u32[]{:S(2)}, u32[]{:S(2)}) async-start(bf16[64,48,128]{2,1,0:T(8,128)(2,1)} %pack_q.1), calls=%async_computation | async-start | bytes 1572864 | tf_op jit(solution)/shard_map/all_to_all | solution.py:390
  63.6 0.7 states.1
  64.4 4.0 %collective-permute-start = (bf16[136,128]{1,0:T(8,128)(2,1)S(1)}, bf16[136,128]{1,0:T(8,128)(2,1)S(1)}, u32[]{:S(2)}, u32[]{:S(2)}) collective-permute-start(bf16[136,128]{1,0:T(8,128)(2,1)S(1)} %convert_element_type.23), channel_id=1, source_target_pairs={{0,64},{64,0},{128,192},{192,128},{256,320},{320,256},{384,448},{4... | collective-permute-start | bytes 104456 | tf_op jit(solution)/shard_map/ppermute | solution.py:366
  68.4 1.6 %collective-permute-done = bf16[136,128]{1,0:T(8,128)(2,1)S(1)} collective-permute-done((bf16[136,128]{1,0:T(8,128)(2,1)S(1)}, bf16[136,128]{1,0:T(8,128)(2,1)S(1)}, u32[]{:S(2)}, u32[]{:S(2)}) %collective-permute-start) | collective-permute-done | bytes 34848 | tf_op jit(solution)/shard_map/ppermute | solution.py:366
  70.1 10.0 %collective-permute-start.1 = (bf16[136,128]{1,0:T(8,128)(2,1)S(1)}, bf16[136,128]{1,0:T(8,128)(2,1)S(1)}, u32[]{:S(2)}, u32[]{:S(2)}) collective-permute-start(bf16[136,128]{1,0:T(8,128)(2,1)S(1)} %pad_maximum_fusion.1), channel_id=1, source_target_pairs={{0,384},{64,448},{128,256},{192,320},{1,385},{65,449},{129,257},{1... | collective-permute-start | bytes 104456 | tf_op jit(solution)/shard_map/ppermute | solution.py:371
  80.1 1.0 collective-permute-done.1
  81.1 2.2 %collective-permute-start.2 = (bf16[272,128]{1,0:T(8,128)(2,1)S(1)}, bf16[272,128]{1,0:T(8,128)(2,1)S(1)}, u32[]{:S(2)}, u32[]{:S(2)}) collective-permute-start(bf16[272,128]{1,0:T(8,128)(2,1)S(1)} %pad_maximum_fusion), channel_id=1, source_target_pairs={{0,128},{64,192},{256,384},{320,448},{384,256},{448,320},{1,129},{... | collective-permute-start | bytes 208904 | tf_op jit(solution)/shard_map/ppermute | solution.py:372
  83.3 1.3 %collective-permute-done.2 = bf16[272,128]{1,0:T(8,128)(2,1)S(1)} collective-permute-done((bf16[272,128]{1,0:T(8,128)(2,1)S(1)}, bf16[272,128]{1,0:T(8,128)(2,1)S(1)}, u32[]{:S(2)}, u32[]{:S(2)}) %collective-permute-start.2) | collective-permute-done | bytes 69664 | tf_op jit(solution)/shard_map/ppermute | solution.py:372
  84.7 1.3 %all-to-all-done.query_ref = bf16[64,48,128]{2,1,0:T(8,128)(2,1)S(1)} async-done(((bf16[64,48,128]{2,1,0:T(8,128)(2,1)}), bf16[64,48,128]{2,1,0:T(8,128)(2,1)S(1)}, u32[]{:S(2)}, u32[]{:S(2)}) %all-to-all-start) | async-done | bytes 786464 | tf_op jit(solution)/shard_map/all_to_all | solution.py:390
  86.0 0.0 copy-start.2
  86.0 1.4 %attend.1 = bf16[64,48,128]{2,1,0:T(8,128)(2,1)S(1)} custom-call(bf16[64,48,128]{2,1,0:T(8,128)(2,1)S(1)} %all-to-all-done.query_ref, bf16[64,104,128]{2,1,0:T(8,128)(2,1)S(1)} %all-to-all-done.1.kv_ref, f32[8,128,128]{2,1,0:T(8,128)S(1)} %get-tuple-element.10.prefix_ref, f32[8,8,384]{2,1,0:T(8,128)S(1)} %get-tuple-element.11.factor_ref, ...), custom_call_target="tpu_custom_call" | custom-call | tf_op jit(solution)/shard_map/attend/pallas_call | solution.py:302
  87.4 33.7 %all_to_all.15.mixed_ref = bf16[64,48,128]{2,1,0:T(8,128)(2,1)S(1)} all-to-all(bf16[64,48,128]{2,1,0:T(8,128)(2,1)S(1)} %attend.1), channel_id=1, replica_groups=mesh['seg'=8,'chip'=4,'core'=2,'head'=8] {'head','core','chip'}, dimensions={0} | all-to-all | bytes 1572864 | tf_op jit(solution)/shard_map/all_to_all | solution.py:394
  121.2 0.0 copy-done.2
  121.2 2.0 %norm.1 = bf16[48,64,128]{2,1,0:T(8,128)(2,1)} custom-call(bf16[64,48,128]{2,1,0:T(8,128)(2,1)S(1)} %all_to_all.15.mixed_ref, f32[64,128]{1,0:T(8,128)S(1)} %copy-done.2), custom_call_target="tpu_custom_call" | custom-call | tf_op jit(solution)/shard_map/norm/pallas_call | solution.py:340
  (11 shorter events, 0.1 us)
Async XLA Ops:
  3.6 11.8 %copy-start = (bf16[48,64,128]{2,1,0:T(8,128)(2,1)S(1)}, bf16[48,64,128]{2,1,0:T(8,128)(2,1)}, u32[]{:S(2)}) copy-start(bf16[48,64,128]{2,1,0:T(8,128)(2,1)} %queries_ref.1) | copy-start | bytes 2359300
  3.6 11.8 %copy-start.1 = (bf16[48,64]{1,0:T(8,128)(2,1)S(1)}, bf16[48,64]{1,0:T(8,128)(2,1)}, u32[]{:S(2)}) copy-start(bf16[48,64]{1,0:T(8,128)(2,1)} %decay_hbm.1) | copy-start | bytes 18436
  3.6 53.1 %all-to-all-start.1 = ((bf16[64,104,128]{2,1,0:T(8,128)(2,1)}), bf16[64,104,128]{2,1,0:T(8,128)(2,1)S(1)}, u32[]{:S(2)}, u32[]{:S(2)}) async-start(bf16[64,104,128]{2,1,0:T(8,128)(2,1)} %pack_kv.1), calls=%async_computation.1 | async-start | bytes 3407872 | tf_op jit(solution)/shard_map/all_to_all | solution.py:388
  56.7 29.3 %all-to-all-start = ((bf16[64,48,128]{2,1,0:T(8,128)(2,1)}), bf16[64,48,128]{2,1,0:T(8,128)(2,1)S(1)}, u32[]{:S(2)}, u32[]{:S(2)}) async-start(bf16[64,48,128]{2,1,0:T(8,128)(2,1)} %pack_q.1), calls=%async_computation | async-start | bytes 1572864 | tf_op jit(solution)/shard_map/all_to_all | solution.py:390
  64.4 5.6 %collective-permute-start = (bf16[136,128]{1,0:T(8,128)(2,1)S(1)}, bf16[136,128]{1,0:T(8,128)(2,1)S(1)}, u32[]{:S(2)}, u32[]{:S(2)}) collective-permute-start(bf16[136,128]{1,0:T(8,128)(2,1)S(1)} %convert_element_type.23), channel_id=1, source_target_pairs={{0,64},{64,0},{128,192},{192,128},{256,320},{320,256},{384,448},{4... | collective-permute-start | bytes 104456 | tf_op jit(solution)/shard_map/ppermute | solution.py:366
  70.1 11.0 %collective-permute-start.1 = (bf16[136,128]{1,0:T(8,128)(2,1)S(1)}, bf16[136,128]{1,0:T(8,128)(2,1)S(1)}, u32[]{:S(2)}, u32[]{:S(2)}) collective-permute-start(bf16[136,128]{1,0:T(8,128)(2,1)S(1)} %pad_maximum_fusion.1), channel_id=1, source_target_pairs={{0,384},{64,448},{128,256},{192,320},{1,385},{65,449},{129,257},{1... | collective-permute-start | bytes 104456 | tf_op jit(solution)/shard_map/ppermute | solution.py:371
  81.1 3.5 %collective-permute-start.2 = (bf16[272,128]{1,0:T(8,128)(2,1)S(1)}, bf16[272,128]{1,0:T(8,128)(2,1)S(1)}, u32[]{:S(2)}, u32[]{:S(2)}) collective-permute-start(bf16[272,128]{1,0:T(8,128)(2,1)S(1)} %pad_maximum_fusion), channel_id=1, source_target_pairs={{0,128},{64,192},{256,384},{320,448},{384,256},{448,320},{1,129},{... | collective-permute-start | bytes 208904 | tf_op jit(solution)/shard_map/ppermute | solution.py:372
  86.0 35.2 %copy-start.2 = (f32[64,128]{1,0:T(8,128)S(1)}, f32[64,128]{1,0:T(8,128)}, u32[]{:S(2)}) copy-start(f32[64,128]{1,0:T(8,128)} %gain_ref.1) | copy-start | bytes 98308

commit v7 on v6

--- a/solution.py
+++ b/solution.py
@@ -368,15 +368,15 @@
     own_decay = own[dim : dim + 1]
     joined = (odd * own_decay + (1.0 - odd)) * state + ((1.0 - odd) * decay + odd) * own[:dim]
     pair = jnp.concatenate([joined, jnp.broadcast_to(decay * own_decay, (EXTRA, dim))], axis=0).astype(BF16)
-    first = lax.ppermute(pair, "seg", [(0, 6), (1, 7), (2, 4), (3, 5)])
+    first = lax.ppermute(pair, "seg", [(0, 4), (1, 5), (2, 6), (3, 7)])
     both = lax.ppermute(
         jnp.concatenate([pair, first], axis=0), "seg", [(0, 2), (1, 3), (4, 6), (5, 7), (6, 4), (7, 5)]
     )
     mine, mine_decay = received(first)
     before, before_decay = received(both[:rows])
     theirs, theirs_decay = received(both[rows:])
-    early = second * mine + (1.0 - second) * theirs
-    late, late_decay = second * theirs + (1.0 - second) * mine, second * theirs_decay + (1.0 - second) * mine_decay
+    early = second * theirs + (1.0 - second) * mine
+    late, late_decay = second * mine + (1.0 - second) * theirs, second * mine_decay + (1.0 - second) * theirs_decay
     state = late + late_decay * early
     state = second * before + (second * before_decay + (1.0 - second)) * state
     return entering_decay * state + entering_state

time: 124 us -> 126 us (1.016)
  starting transfers between devices: 34.8 us -> 36.8 us
  blocking collectives: 33.7 us -> 35.1 us
  waiting for transfers between devices: 42.2 us -> 40.9 us
    ppermute x1, starting transfers between devices: 2.16 us -> 4.19 us  [incoming_state(): lax.ppermute(jnp.concatenate([pair, first], axis=0), 'seg', [(0, 2), (1,...]
    all_to_all x1, blocking collectives: 33.7 us -> 35.1 us  [shards(): mixed = lax.all_to_all(mixed, group, 0, 0, tiled=True)]
    all_to_all x1, waiting for transfers between devices: 1.28 us -> 0.01 us  [shards(): query = lax.all_to_all(query, group, 0, 0, tiled=True)]
  transfers between devices with their start and end apart: 5 -> 5, of which waited for: 5 -> 4; matrix products, arithmetic and copies ran while one was open for 0% -> 0% of each run, Pallas kernels for 4% -> 4%
where the time goes in v7:
time: 126 us; the launch traced here: 125 us
  waiting for transfers between devices  40.9 us (32%)
  starting transfers between devices  36.8 us (29%)
  blocking collectives  35.1 us (28%)
  Pallas kernels  12.1 us (10%)
    all_to_all x1, waiting for transfers between devices, shards(): lax.all_to_all(pack_kv(keys, values, decay_log), group, 0, 0, tiled=True)  36.9 us
    all_to_all x1, blocking collectives, shards(): mixed = lax.all_to_all(mixed, group, 0, 0, tiled=True)  35.1 us
    all_to_all x1, starting transfers between devices, shards(): lax.all_to_all(pack_kv(keys, values, decay_log), group, 0, 0, tiled=True)  11.8 us
    ppermute x1, starting transfers between devices, incoming_state(): first = lax.ppermute(pair, 'seg', [(0, 4), (1, 5), (2, 6), (3, 7)])  10 us
    all_to_all x1, starting transfers between devices, shards(): query = lax.all_to_all(query, group, 0, 0, tiled=True)  6.9 us
    pallas_call x1, Pallas kernels, pack_q(): pl.pallas_call(pack_q_kernel, grid=(heads // 8,), in_specs=[pl.BlockSpec(...  4.4 us
    ppermute x1, starting transfers between devices, incoming_state(): lax.ppermute(jnp.concatenate([pair, first], axis=0), 'seg', [(0, 2), (1,...  4.19 us
    ppermute x1, starting transfers between devices, incoming_state(): lax.ppermute(own.astype(BF16), 'seg', [(i, i ^ 1) for i in range(8)])  3.99 us
  transfers between devices with their start and end apart: 5, of which 4 were waited for; matrix products, arithmetic and copies ran while one was open for 0% of the time, Pallas kernels for 4%

profile of v7, /device:TPU:1, one launch (start us, length us, event | category | flops | bytes accessed | tf_op | source)
XLA Modules:
  0.0 125.2 jit_solution(17474600006943051136)
XLA Ops:
  0.0 3.5 %pack_kv.1 = bf16[64,104,128]{2,1,0:T(8,128)(2,1)} custom-call(bf16[48,64]{1,0:T(8,128)(2,1)} %decay_hbm.1, bf16[48,64,128]{2,1,0:T(8,128)(2,1)} %keys_hbm.1, bf16[48,64,128]{2,1,0:T(8,128)(2,1)} %values_hbm.1), custom_call_target="tpu_custom_call" | custom-call | tf_op jit(solution)/shard_map/pack_kv/pallas_call | solution.py:111
  3.6 0.0 copy-start
  3.6 0.0 copy-start.1
  3.6 11.8 %all-to-all-start.1 = ((bf16[64,104,128]{2,1,0:T(8,128)(2,1)}), bf16[64,104,128]{2,1,0:T(8,128)(2,1)S(1)}, u32[]{:S(2)}, u32[]{:S(2)}) async-start(bf16[64,104,128]{2,1,0:T(8,128)(2,1)} %pack_kv.1), calls=%async_computation.1 | async-start | bytes 3407872 | tf_op jit(solution)/shard_map/all_to_all | solution.py:388
  15.4 0.0 copy-done
  15.4 0.0 copy-done.1
  15.4 4.4 %pack_q.1 = bf16[64,48,128]{2,1,0:T(8,128)(2,1)} custom-call(bf16[48,64]{1,0:T(8,128)(2,1)S(1)} %copy-done.1, bf16[48,64,128]{2,1,0:T(8,128)(2,1)S(1)} %copy-done), custom_call_target="tpu_custom_call" | custom-call | tf_op jit(solution)/shard_map/pack_q/pallas_call | solution.py:146
  19.8 36.9 %all-to-all-done.1.kv_ref = bf16[64,104,128]{2,1,0:T(8,128)(2,1)S(1)} async-done(((bf16[64,104,128]{2,1,0:T(8,128)(2,1)}), bf16[64,104,128]{2,1,0:T(8,128)(2,1)S(1)}, u32[]{:S(2)}, u32[]{:S(2)}) %all-to-all-start.1) | async-done | bytes 1703968 | tf_op jit(solution)/shard_map/all_to_all | solution.py:388
  56.7 6.9 %all-to-all-start = ((bf16[64,48,128]{2,1,0:T(8,128)(2,1)}), bf16[64,48,128]{2,1,0:T(8,128)(2,1)S(1)}, u32[]{:S(2)}, u32[]{:S(2)}) async-start(bf16[64,48,128]{2,1,0:T(8,128)(2,1)} %pack_q.1), calls=%async_computation | async-start | bytes 1572864 | tf_op jit(solution)/shard_map/all_to_all | solution.py:390
  63.6 0.7 states.1
  64.4 4.0 %collective-permute-start = (bf16[136,128]{1,0:T(8,128)(2,1)S(1)}, bf16[136,128]{1,0:T(8,128)(2,1)S(1)}, u32[]{:S(2)}, u32[]{:S(2)}) collective-permute-start(bf16[136,128]{1,0:T(8,128)(2,1)S(1)} %convert_element_type.23), channel_id=1, source_target_pairs={{0,64},{64,0},{128,192},{192,128},{256,320},{320,256},{384,448},{4... | collective-permute-start | bytes 104456 | tf_op jit(solution)/shard_map/ppermute | solution.py:366
  68.4 1.6 %collective-permute-done = bf16[136,128]{1,0:T(8,128)(2,1)S(1)} collective-permute-done((bf16[136,128]{1,0:T(8,128)(2,1)S(1)}, bf16[136,128]{1,0:T(8,128)(2,1)S(1)}, u32[]{:S(2)}, u32[]{:S(2)}) %collective-permute-start) | collective-permute-done | bytes 34848 | tf_op jit(solution)/shard_map/ppermute | solution.py:366
  70.1 10.0 %collective-permute-start.1 = (bf16[136,128]{1,0:T(8,128)(2,1)S(1)}, bf16[136,128]{1,0:T(8,128)(2,1)S(1)}, u32[]{:S(2)}, u32[]{:S(2)}) collective-permute-start(bf16[136,128]{1,0:T(8,128)(2,1)S(1)} %pad_maximum_fusion.1), channel_id=1, source_target_pairs={{0,256},{64,320},{128,384},{192,448},{1,257},{65,321},{129,385},{1... | collective-permute-start | bytes 104456 | tf_op jit(solution)/shard_map/ppermute | solution.py:371
  80.1 1.0 collective-permute-done.1
  81.1 4.2 %collective-permute-start.2 = (bf16[272,128]{1,0:T(8,128)(2,1)S(1)}, bf16[272,128]{1,0:T(8,128)(2,1)S(1)}, u32[]{:S(2)}, u32[]{:S(2)}) collective-permute-start(bf16[272,128]{1,0:T(8,128)(2,1)S(1)} %pad_maximum_fusion), channel_id=1, source_target_pairs={{0,128},{64,192},{256,384},{320,448},{384,256},{448,320},{1,129},{... | collective-permute-start | bytes 208904 | tf_op jit(solution)/shard_map/ppermute | solution.py:372
  85.3 1.3 %collective-permute-done.2 = bf16[272,128]{1,0:T(8,128)(2,1)S(1)} collective-permute-done((bf16[272,128]{1,0:T(8,128)(2,1)S(1)}, bf16[272,128]{1,0:T(8,128)(2,1)S(1)}, u32[]{:S(2)}, u32[]{:S(2)}) %collective-permute-start.2) | collective-permute-done | bytes 69664 | tf_op jit(solution)/shard_map/ppermute | solution.py:372
  86.7 0.0 all-to-all-done.query_ref
  86.7 0.0 copy-start.2
  86.7 1.4 %attend.1 = bf16[64,48,128]{2,1,0:T(8,128)(2,1)S(1)} custom-call(bf16[64,48,128]{2,1,0:T(8,128)(2,1)S(1)} %all-to-all-done.query_ref, bf16[64,104,128]{2,1,0:T(8,128)(2,1)S(1)} %all-to-all-done.1.kv_ref, f32[8,128,128]{2,1,0:T(8,128)S(1)} %get-tuple-element.10.prefix_ref, f32[8,8,384]{2,1,0:T(8,128)S(1)} %get-tuple-element.11.factor_ref, ...), custom_call_target="tpu_custom_call" | custom-call | tf_op jit(solution)/shard_map/attend/pallas_call | solution.py:302
  88.2 35.1 %all_to_all.15.mixed_ref = bf16[64,48,128]{2,1,0:T(8,128)(2,1)S(1)} all-to-all(bf16[64,48,128]{2,1,0:T(8,128)(2,1)S(1)} %attend.1), channel_id=1, replica_groups=mesh['seg'=8,'chip'=4,'core'=2,'head'=8] {'head','core','chip'}, dimensions={0} | all-to-all | bytes 1572864 | tf_op jit(solution)/shard_map/all_to_all | solution.py:394
  123.2 0.0 copy-done.2
  123.2 2.0 %norm.1 = bf16[48,64,128]{2,1,0:T(8,128)(2,1)} custom-call(bf16[64,48,128]{2,1,0:T(8,128)(2,1)S(1)} %all_to_all.15.mixed_ref, f32[64,128]{1,0:T(8,128)S(1)} %copy-done.2), custom_call_target="tpu_custom_call" | custom-call | tf_op jit(solution)/shard_map/norm/pallas_call | solution.py:340
  (11 shorter events, 0.1 us)
Async XLA Ops:
  3.6 11.8 %copy-start = (bf16[48,64,128]{2,1,0:T(8,128)(2,1)S(1)}, bf16[48,64,128]{2,1,0:T(8,128)(2,1)}, u32[]{:S(2)}) copy-start(bf16[48,64,128]{2,1,0:T(8,128)(2,1)} %queries_ref.1) | copy-start | bytes 2359300
  3.6 11.8 %copy-start.1 = (bf16[48,64]{1,0:T(8,128)(2,1)S(1)}, bf16[48,64]{1,0:T(8,128)(2,1)}, u32[]{:S(2)}) copy-start(bf16[48,64]{1,0:T(8,128)(2,1)} %decay_hbm.1) | copy-start | bytes 18436
  3.6 53.1 %all-to-all-start.1 = ((bf16[64,104,128]{2,1,0:T(8,128)(2,1)}), bf16[64,104,128]{2,1,0:T(8,128)(2,1)S(1)}, u32[]{:S(2)}, u32[]{:S(2)}) async-start(bf16[64,104,128]{2,1,0:T(8,128)(2,1)} %pack_kv.1), calls=%async_computation.1 | async-start | bytes 3407872 | tf_op jit(solution)/shard_map/all_to_all | solution.py:388
  56.7 30.0 %all-to-all-start = ((bf16[64,48,128]{2,1,0:T(8,128)(2,1)}), bf16[64,48,128]{2,1,0:T(8,128)(2,1)S(1)}, u32[]{:S(2)}, u32[]{:S(2)}) async-start(bf16[64,48,128]{2,1,0:T(8,128)(2,1)} %pack_q.1), calls=%async_computation | async-start | bytes 1572864 | tf_op jit(solution)/shard_map/all_to_all | solution.py:390
  64.4 5.6 %collective-permute-start = (bf16[136,128]{1,0:T(8,128)(2,1)S(1)}, bf16[136,128]{1,0:T(8,128)(2,1)S(1)}, u32[]{:S(2)}, u32[]{:S(2)}) collective-permute-start(bf16[136,128]{1,0:T(8,128)(2,1)S(1)} %convert_element_type.23), channel_id=1, source_target_pairs={{0,64},{64,0},{128,192},{192,128},{256,320},{320,256},{384,448},{4... | collective-permute-start | bytes 104456 | tf_op jit(solution)/shard_map/ppermute | solution.py:366
  70.1 11.0 %collective-permute-start.1 = (bf16[136,128]{1,0:T(8,128)(2,1)S(1)}, bf16[136,128]{1,0:T(8,128)(2,1)S(1)}, u32[]{:S(2)}, u32[]{:S(2)}) collective-permute-start(bf16[136,128]{1,0:T(8,128)(2,1)S(1)} %pad_maximum_fusion.1), channel_id=1, source_target_pairs={{0,256},{64,320},{128,384},{192,448},{1,257},{65,321},{129,385},{1... | collective-permute-start | bytes 104456 | tf_op jit(solution)/shard_map/ppermute | solution.py:371
  81.1 5.5 %collective-permute-start.2 = (bf16[272,128]{1,0:T(8,128)(2,1)S(1)}, bf16[272,128]{1,0:T(8,128)(2,1)S(1)}, u32[]{:S(2)}, u32[]{:S(2)}) collective-permute-start(bf16[272,128]{1,0:T(8,128)(2,1)S(1)} %pad_maximum_fusion), channel_id=1, source_target_pairs={{0,128},{64,192},{256,384},{320,448},{384,256},{448,320},{1,129},{... | collective-permute-start | bytes 208904 | tf_op jit(solution)/shard_map/ppermute | solution.py:372
  86.7 36.5 %copy-start.2 = (f32[64,128]{1,0:T(8,128)S(1)}, f32[64,128]{1,0:T(8,128)}, u32[]{:S(2)}) copy-start(f32[64,128]{1,0:T(8,128)} %gain_ref.1) | copy-start | bytes 98308
